TPU v7x, 128 devices: a whole 4x4x4 slice. The times are simulated.
128 devices in a mesh: dp: 4 (over x), expert: 32 (over y, z, core).
Axes of the slice: x: 4, y: 4, z: 4, core: 2. Of those that a mesh axis runs over, the one named last changes fastest.
Arguments:
- hidden: bfloat16 [16384, 2880], P(('dp', 'expert')), may hold values from -12 to 12
- query_base_rows: bfloat16 [16384, 2048], P(('dp', 'expert')), may hold values from -17 to 17
- key_base_rows: bfloat16 [16384, 256], P(('dp', 'expert')), may hold values from -17 to 17
- value_base_rows: bfloat16 [16384, 256], P(('dp', 'expert')), may hold values from -6 to 6
- prompt_number: int32 [4, 4096], P('dp', 'expert'), may hold values from 0 to 15, never falling along the last dimension, each value on 1 to 2048 neighbouring positions
- prompt_adapter: int32 [4, 16], P('dp'), may hold values from 0 to 15
- sinks: float32 [32], replicated, may hold values from 0 to 3
- attention_gain: float32 [2880], replicated, may hold values from 0.5 to 1.5
- adapter_down_factors: bfloat16 [16, 48, 2880], P('dp'), may hold values from -0.109375 to 0.109375
- query_up_factors: bfloat16 [16, 16, 2048], P('dp'), may hold values from -1.5 to 1.5
- key_value_up_factors: bfloat16 [16, 16, 512], P('dp'), may hold values from -1.5 to 1.5
- output_down_factors: bfloat16 [16, 16, 2048], P('dp'), may hold values from -0.125 to 0.125
- output_up_factors: bfloat16 [16, 16, 2880], P('dp'), may hold values from -1.5 to 1.5
- attention_output_weight: bfloat16 [2048, 2880], replicated, may hold values from -0.125 to 0.125
- expert_norm_gain: float32 [2880], replicated, may hold values from 0.5 to 1.5
- expert_gate_up_weight: bfloat16 [32, 1536, 2, 2880], P('expert', 'dp'), may hold values from -0.109375 to 0.109375
- expert_down_weight: bfloat16 [32, 1536, 2880], P('expert', 'dp'), may hold values from -0.15625 to 0.15625
- routes: int32 [16384, 4], P(('dp', 'expert')), may hold values from 0 to 31, all different within a row; in each aligned block of 128 rows (0 to 127, 128 to 255, ...) at most 20 rows name the same one
- routing_gate_weight: float32 [16384, 4], P(('dp', 'expert')), may hold values from 0.05 to 0.5
Outputs:
- layer_out: bfloat16 [16384, 2880], P(('dp', 'expert'))
Inputs may be any that keep to these rules, and one draw needn't show every extreme that they name: `routes`: among the rows of one device, no expert is named by more than 20 rows. `prompt_number`: in each request group, prompt numbers never fall along the tokens, and every prompt has at most half of 4096 tokens.
All inputs are finite; a program needn't handle non-finite values.
Results may differ from a plain program's by a relative error of at most 0.0098.
The roundings to bfloat16 on the way count: a program that leaves them out, or rounds other values in their place, can miss the bound.
Values may be sent and summed in bfloat16 or wider, within the bound.
A program may use at most 256 MiB of HBM per device.

v0:
```python
import jax
import jax.numpy as jnp
from jax import lax
from jax.sharding import PartitionSpec as P

HD = 64
ADAPTER_RANK = 16
TOP = 4


EPSILON = 1e-05
ROPE_BASE = 150000.0
SCORE_SCALE = 0.125
NEGATIVE = -1e30


def rms_scale(rows_in, gain):
    floats = rows_in.astype(jnp.float32)
    mean_square = jnp.mean(floats * floats, axis=-1, keepdims=True)
    return (floats * lax.rsqrt(mean_square + EPSILON) * gain).astype(jnp.bfloat16)


def rotate(heads, positions):
    head_dim = heads.shape[-1]
    half = head_dim // 2
    freqs = ROPE_BASE ** (-(2.0 * jnp.arange(half, dtype=jnp.float32) / head_dim))
    angle = positions.astype(jnp.float32)[:, None] * freqs[None, :]
    cosine = jnp.cos(angle)[:, None, :]
    sine = jnp.sin(angle)[:, None, :]
    first = heads[..., :half]
    second = heads[..., half:]
    return jnp.concatenate(
        [first * cosine - second * sine, second * cosine + first * sine], axis=-1
    )


def multiply_rows(left, right):
    return lax.dot_general(
        left, right, (((1,), (1,)), ((), ())), preferred_element_type=jnp.float32
    )


def select_adapter(all_terms, adapter_selector, span):
    stacked = all_terms.reshape(all_terms.shape[0], adapter_selector.shape[1], span)
    return jnp.sum(stacked * adapter_selector[:, :, None], axis=1)


def spread(adapter_selector, low_part):
    joined = adapter_selector[:, :, None] * low_part.astype(jnp.float32)[:, None, :]
    return joined.reshape(joined.shape[0], -1).astype(jnp.bfloat16)


def expert_hidden(rows_in, gate_up):
    gate_out = multiply_rows(rows_in, gate_up[:, 0, :])
    up_out = multiply_rows(rows_in, gate_up[:, 1, :])
    return (jax.nn.silu(gate_out) * up_out).astype(jnp.bfloat16)


def shards(
    hidden,
    query_base_rows,
    key_base_rows,
    value_base_rows,
    prompt_number,
    prompt_adapter,
    sinks,
    attention_gain,
    adapter_down_factors,
    query_up_factors,
    key_value_up_factors,
    output_down_factors,
    output_up_factors,
    attention_output_weight,
    expert_norm_gain,
    expert_gate_up_weight,
    expert_down_weight,
    routes,
    routing_gate_weight,
):
    tok_rows = hidden.shape[0]
    model_width = hidden.shape[1]
    q_width = query_base_rows.shape[1]
    kv_width = key_base_rows.shape[1]
    kv_heads = kv_width // HD
    groups = q_width // HD // kv_heads
    doc_count = prompt_adapter.shape[1]
    row_ids = lax.all_gather(prompt_number, "expert", axis=1, tiled=True)[0]
    my_ids = prompt_number[0]
    doc_range = jnp.arange(doc_count, dtype=jnp.int32)
    counts = jnp.sum((row_ids[:, None] == doc_range[None, :]).astype(jnp.int32), axis=0)
    firsts = jnp.cumsum(counts) - counts
    doc_hot = (my_ids[:, None] == doc_range[None, :]).astype(jnp.int32)
    query_index = lax.axis_index("expert") * tok_rows + jnp.arange(tok_rows, dtype=jnp.int32)
    positions = query_index - jnp.sum(doc_hot * firsts[None, :], axis=1)
    adapter_of = jnp.sum(doc_hot * prompt_adapter[0][None, :], axis=1)
    factors = (
        lax.all_gather(adapter_down_factors, "dp", axis=0, tiled=True),
        lax.all_gather(query_up_factors, "dp", axis=0, tiled=True),
        lax.all_gather(key_value_up_factors, "dp", axis=0, tiled=True),
        lax.all_gather(output_down_factors, "dp", axis=0, tiled=True),
        lax.all_gather(output_up_factors, "dp", axis=0, tiled=True),
    )
    all_down, all_up_query, all_up_keyval, all_o_down, all_o_up = factors
    adapter_table = all_down.shape[0]
    adapter_selector = (
        adapter_of[:, None] == jnp.arange(adapter_table, dtype=jnp.int32)[None, :]
    ).astype(jnp.float32)
    normalized_tokens = rms_scale(hidden, attention_gain)
    lowrank_part = select_adapter(
        multiply_rows(
            normalized_tokens, all_down.reshape(adapter_table * 3 * ADAPTER_RANK, model_width)
        ),
        adapter_selector,
        3 * ADAPTER_RANK,
    ).astype(jnp.bfloat16)
    q_delta = jnp.dot(
        spread(adapter_selector, lowrank_part[:, :ADAPTER_RANK]),
        all_up_query.reshape(adapter_table * ADAPTER_RANK, q_width),
        preferred_element_type=jnp.float32,
    )
    k_delta = jnp.dot(
        spread(adapter_selector, lowrank_part[:, ADAPTER_RANK : 2 * ADAPTER_RANK]),
        all_up_keyval[:, :, :kv_width].reshape(adapter_table * ADAPTER_RANK, kv_width),
        preferred_element_type=jnp.float32,
    )
    v_delta = jnp.dot(
        spread(adapter_selector, lowrank_part[:, 2 * ADAPTER_RANK :]),
        all_up_keyval[:, :, kv_width:].reshape(adapter_table * ADAPTER_RANK, kv_width),
        preferred_element_type=jnp.float32,
    )
    queries = rotate(
        (query_base_rows.astype(jnp.float32) + q_delta).reshape(tok_rows, kv_heads * groups, HD),
        positions,
    )
    queries = queries.astype(jnp.bfloat16).reshape(tok_rows, kv_heads, groups, HD)
    key_rows = rotate(
        (key_base_rows.astype(jnp.float32) + k_delta).reshape(tok_rows, kv_heads, HD), positions
    )
    key_rows = key_rows.astype(jnp.bfloat16).reshape(tok_rows, kv_width)
    value_rows = (value_base_rows.astype(jnp.float32) + v_delta).astype(jnp.bfloat16)
    sink_grid = sinks.reshape(kv_heads, groups)
    running_max = jnp.broadcast_to(sink_grid[:, :, None], (kv_heads, groups, tok_rows))
    running_sum = jnp.ones((kv_heads, groups, tok_rows), jnp.float32)
    weighted = jnp.zeros((kv_heads, groups, tok_rows, HD), jnp.float32)
    piece_keys = lax.all_gather(key_rows, "expert", axis=0, tiled=True)
    piece_values = lax.all_gather(value_rows, "expert", axis=0, tiled=True)
    piece_rows = piece_keys.shape[0]
    piece_keys = piece_keys.reshape(piece_rows, kv_heads, HD)
    piece_values = piece_values.reshape(piece_rows, kv_heads, HD)
    key_index = jnp.arange(piece_rows, dtype=jnp.int32)
    scores = (
        jnp.einsum("tkgd,nkd->kgtn", queries, piece_keys, preferred_element_type=jnp.float32)
        * SCORE_SCALE
    )
    allowed = (key_index[None, :] <= query_index[:, None]) & (row_ids[None, :] == my_ids[:, None])
    scores = jnp.where(allowed[None, None], scores, NEGATIVE)
    fresh_max = jnp.maximum(running_max, jnp.max(scores, axis=-1))
    exps = jnp.exp(scores - fresh_max[..., None])
    factor = jnp.exp(running_max - fresh_max)
    running_sum = running_sum * factor + jnp.sum(exps, axis=-1)
    weighted = weighted * factor[..., None] + jnp.einsum(
        "kgtn,nkd->kgtd",
        exps.astype(jnp.bfloat16),
        piece_values,
        preferred_element_type=jnp.float32,
    )
    attended = (
        jnp.transpose(weighted / running_sum[..., None], (2, 0, 1, 3))
        .reshape(tok_rows, q_width)
        .astype(jnp.bfloat16)
    )
    o_low = select_adapter(
        multiply_rows(attended, all_o_down.reshape(adapter_table * ADAPTER_RANK, q_width)),
        adapter_selector,
        ADAPTER_RANK,
    ).astype(jnp.bfloat16)
    projected = jnp.dot(attended, attention_output_weight, preferred_element_type=jnp.float32)
    projected = projected + jnp.dot(
        spread(adapter_selector, o_low),
        all_o_up.reshape(adapter_table * ADAPTER_RANK, model_width),
        preferred_element_type=jnp.float32,
    )
    mid = (hidden.astype(jnp.float32) + projected).astype(jnp.bfloat16)
    moe_in = rms_scale(mid, expert_norm_gain)
    exp_dev = expert_gate_up_weight.shape[0]
    experts = lax.axis_size("expert") * exp_dev
    capacity = 5 * tok_rows * TOP // (4 * experts)
    flat_routes = routes.reshape(tok_rows * TOP)
    route_hot = (flat_routes[:, None] == jnp.arange(experts, dtype=jnp.int32)[None, :]).astype(
        jnp.int32
    )
    before = jnp.cumsum(route_hot, axis=0) - route_hot
    slot_index = jnp.sum(before * route_hot, axis=1)
    buffer_index = flat_routes * capacity + slot_index
    source = (
        jnp.full((experts * capacity,), -1, jnp.int32)
        .at[buffer_index]
        .set(jnp.arange(tok_rows * TOP, dtype=jnp.int32))
    )
    filled = source >= 0
    picked = jnp.take(moe_in, jnp.maximum(source, 0) // TOP, axis=0)
    dispatch = jnp.where(filled[:, None], picked, jnp.zeros_like(picked)).reshape(
        experts, capacity, model_width
    )
    arrived = lax.all_to_all(dispatch, "expert", split_axis=0, concat_axis=0, tiled=True)
    sender_rows = arrived.shape[0]
    item_count = arrived.shape[1]
    gathered = lax.all_gather(arrived, "dp", axis=0, tiled=True)
    row_count = sender_rows * lax.axis_size("dp")
    grouped = gathered.reshape(row_count // exp_dev, exp_dev, item_count, model_width)
    flat_rows = grouped[:, 0].reshape(-1, model_width)
    activation = expert_hidden(flat_rows, expert_gate_up_weight[0])
    product = jnp.dot(activation, expert_down_weight[0], preferred_element_type=jnp.float32)
    outputs = [product.reshape(row_count // exp_dev, item_count, model_width)]
    summed = lax.psum_scatter(
        jnp.stack(outputs, axis=1).reshape(row_count, item_count, model_width).astype(jnp.bfloat16),
        "dp",
        scatter_dimension=0,
        tiled=True,
    )
    returned = lax.all_to_all(summed, "expert", split_axis=0, concat_axis=0, tiled=True)
    chosen = jnp.take(returned.reshape(experts * capacity, model_width), buffer_index, axis=0)
    scaled = chosen.astype(jnp.float32) * routing_gate_weight.reshape(tok_rows * TOP)[:, None]
    moe = jnp.sum(scaled.reshape(tok_rows, TOP, model_width), axis=1)
    return (mid.astype(jnp.float32) + moe).astype(jnp.bfloat16)


def solution(mesh):
    placed = (
        P(("dp", "expert"), None),
        P(("dp", "expert"), None),
        P(("dp", "expert"), None),
        P(("dp", "expert"), None),
        P("dp", "expert"),
        P("dp", None),
        P(),
        P(),
        P("dp", None, None),
        P("dp", None, None),
        P("dp", None, None),
        P("dp", None, None),
        P("dp", None, None),
        P(),
        P(),
        P("expert", "dp", None, None),
        P("expert", "dp", None),
        P(("dp", "expert"), None),
        P(("dp", "expert"), None),
    )
    return jax.shard_map(
        shards, mesh=mesh, in_specs=placed, out_specs=P(("dp", "expert"), None), check_vma=False
    )
```

profile of v0, /device:TPU:1, one launch (start us, length us, event | category | flops | bytes accessed | tf_op | source)
XLA Modules:
  0.0 782.3 jit_solution(1189234769531826165)
XLA Ops:
  8.1 24.3 %all_gather.29 = s32[1,4096]{1,0:T(1,128)S(1)} all-gather(s32[1,128]{1,0:T(1,128)} %param.23), channel_id=1, replica_groups=mesh['dp'=4,'expert'=32] {'expert'}, dimensions={1}, use_global_device_ids=true | all-gather | bytes 16896 | tf_op jit(solution)/shard_map/all_gather | solution.py:87
  35.1 12.8 %all_gather.32 = bf16[16,16,512]{2,1,0:T(8,128)(2,1)S(1)} all-gather(bf16[4,16,512]{2,1,0:T(8,128)(2,1)} %param.29), channel_id=1, replica_groups=mesh['dp'=4,'expert'=32] {'dp'}, dimensions={0}, use_global_device_ids=true | all-gather | bytes 327680 | tf_op jit(solution)/shard_map/all_gather | solution.py:99
  48.2 16.9 %all-gather.8.cloned.1.call-done = bf16[16,48,2880]{2,1,0:T(8,128)(2,1)} async-done(((bf16[4,48,2880]{2,1,0:T(8,128)(2,1)}), bf16[16,48,2880]{2,1,0:T(8,128)(2,1)}) %all-gather.8.cloned.1.call-update) | async-done | bytes 4423696 | tf_op jit(solution)/shard_map/all_gather | solution.py:97
  65.1 4.0 fusion.31
  79.9 9.4 %all-gather.12.cloned.1.call-done = bf16[16,16,2048]{2,1,0:T(8,128)(2,1)} async-done(((bf16[4,16,2048]{2,1,0:T(8,128)(2,1)}), bf16[16,16,2048]{2,1,0:T(8,128)(2,1)}) %all-gather.12.cloned.1.call-update) | async-done | bytes 1048592 | tf_op jit(solution)/shard_map/all_gather | solution.py:98
  95.8 43.3 %all-gather.10.cloned.1.call-done = bf16[4096,256]{0,1:T(8,128)(2,1)} async-done(((bf16[128,256]{0,1:T(8,128)(2,1)}), bf16[4096,256]{0,1:T(8,128)(2,1)}) %all-gather.10.cloned.1.call-update) | async-done | bytes 2097168 | tf_op jit(solution)/shard_map/all_gather | solution.py:145
  139.1 25.3 %fusion.2 = (f32[4,8,128]{2,1,0:T(8,128)S(1)}, f32[4,4096,128,8]{2,1,3,0:T(8,128)}) fusion(pred[128,4096]{0,1:T(8,128)(4,1)S(1)} %fusion.14, bf16[4096,4,64,1]{0,2,3,1:T(8,128)(2,1)} %bitcast.122, bf16[128,4,8,32]{0,3,2,1:T(8,128)(2,1)S(1)} %bitcast.125, bf16[128,4,8,32]{0,3,2,1:T(8,128)(2,1)S(1)} %bitcast.124), kind=kOutput, calls=%fused_computation.7 | convolution fusion | flops 2198859776 | bytes 70270976 | tf_op jit(solution)/shard_map/tkgd,nkd->kgtn/dot_general | solution.py:152
  164.5 21.9 %fusion = f32[4,8,128]{2,1,0:T(8,128)S(1)} fusion(f32[4,4096,128,8]{2,1,3,0:T(8,128)} %get-tuple-element.22, f32[4,8,128]{2,1,0:T(8,128)S(1)} %broadcast_maximum_fusion, pred[128,4096]{0,1:T(8,128)(4,1)S(1)} %fusion.14), kind=kLoop, calls=%fused_computation.5 | loop fusion | flops 67104768 | bytes 67665920 | tf_op jit(solution)/shard_map/reduce_sum | solution.py:160
  186.5 4.2 copy.80
  190.7 25.5 %fusion.28 = bf16[128,4,8,64]{0,3,2,1:T(8,128)(2,1)S(1)} fusion(bf16[4096,4,64,1]{0,2,3,1:T(8,128)(2,1)} %bitcast.123, f32[4,4096,128,8]{2,1,3,0:T(8,128)} %get-tuple-element.22, f32[4,8,128]{2,1,0:T(8,128)S(1)} %broadcast_maximum_fusion, pred[128,4096]{0,1:T(8,128)(4,1)S(1)} %fusion.14, f32[128,4,8]{0,2,1:T(8,128)S(1)} %get-tuple-element.14, ...), kind=kOutput, calls=%fused_computation.40 | convolution fusion | flops 2215378944 | bytes 70303744 | tf_op jit(solution)/shard_map/kgtn,nkd->kgtd/dot_general | solution.py:161
  218.7 9.2 %fusion.65 = f32[128,2880]{0,1:T(8,128)} fusion(bf16[2048,2880]{0,1:T(8,128)(2,1)} %param.32, bf16[128,2048]{0,1:T(8,128)(2,1)} %bitcast.142), kind=kOutput, calls=%fused_computation.125 | convolution fusion | flops 1509949440 | bytes 13795328 | tf_op jit(solution)/shard_map/dot_general | solution.py:177
  228.0 8.4 %all-gather.18.cloned.1.call-done = bf16[16,16,2880]{2,1,0:T(8,128)(2,1)} async-done(((bf16[4,16,2880]{2,1,0:T(8,128)(2,1)}), bf16[16,16,2880]{2,1,0:T(8,128)(2,1)}) %all-gather.18.cloned.1.call-update) | async-done | bytes 1474576 | tf_op jit(solution)/shard_map/all_gather | solution.py:101
  242.9 4.6 gather_fusion
  247.5 6.4 gather.13
  256.7 62.3 %all_to_all.10 = bf16[32,20,2880]{2,1,0:T(8,128)(2,1)S(1)} all-to-all(bf16[32,20,2880]{2,1,0:T(8,128)(2,1)S(1)} %select_select_fusion), channel_id=1, replica_groups=mesh['dp'=4,'expert'=32] {'expert'}, dimensions={0} | all-to-all | bytes 7372800 | tf_op jit(solution)/shard_map/all_to_all | solution.py:205
  321.3 135.6 %all-gather.20.cloned.1.call-done = bf16[128,20,2880]{2,0,1:T(8,128)(2,1)} async-done(((bf16[32,20,2880]{2,0,1:T(8,128)(2,1)}), bf16[128,20,2880]{2,0,1:T(8,128)(2,1)}) %all-gather.20.cloned.1.call-update) | async-done | bytes 14745616 | tf_op jit(solution)/shard_map/all_gather | solution.py:208
  456.9 16.0 %copy.91 = bf16[128,20,2880]{2,1,0:T(8,128)(2,1)} copy(bf16[128,20,2880]{2,0,1:T(8,128)(2,1)} %all-gather.20.cloned.1.call-done) | data formatting | bytes 29491200 | tf_op jit(solution)/shard_map/all_gather | solution.py:208
  472.8 21.2 %reshape_squeeze_reshape.3 = bf16[2560,2880]{1,0:T(8,128)(2,1)} reshape(bf16[128,20,2880]{2,1,0:T(8,128)(2,1)} %copy.91) | data formatting | bytes 29491200 | tf_op jit(solution)/shard_map/reshape;squeeze;reshape | solution.py:211
  494.1 12.6 %fusion.12 = f32[2560,384]{1,0:T(8,128)S(1)} fusion(bf16[2560,2880]{1,0:T(8,128)(2,1)} %reshape_squeeze_reshape.3, bf16[384,2,2880]{0,2,1:T(8,128)(2,1)} %bitcast.137), kind=kOutput, calls=%fused_computation.24 | convolution fusion | flops 5662310400 | bytes 21217280 | tf_op jit(solution)/shard_map/dot_general | solution.py:38
  506.7 9.7 %fusion.6 = bf16[2560,384]{1,0:T(8,128)(2,1)} fusion(bf16[2560,2880]{1,0:T(8,128)(2,1)S(1)} %copy-done.1, f32[2560,384]{1,0:T(8,128)S(1)} %fusion.12, bf16[384,2,2880]{0,2,1:T(8,128)(2,1)S(1)} %bitcast.140), kind=kOutput, calls=%fused_computation.14 | convolution fusion | flops 5668208640 | bytes 23183360 | tf_op jit(solution)/shard_map/dot_general | solution.py:38
  516.4 4.0 dot_general.52
  520.4 12.6 %convolution_convert_fusion = bf16[128,20,2880]{2,0,1:T(8,128)(2,1)} fusion(bf16[1,384,2880]{1,2,0:T(8,128)(2,1)S(1)} %copy-done, bf16[128,20,384]{2,1,0:T(8,128)(2,1)} %dot_general.52), kind=kOutput, calls=%fused_computation.10 | convolution fusion | flops 5669683200 | bytes 18923520 | tf_op jit(solution)/shard_map/dot_general | solution.py:213
  533.0 135.9 %reduce-scatter.2.cloned.1.call-done = bf16[32,20,2880]{2,0,1:T(8,128)(2,1)} async-done(((bf16[128,20,2880]{2,0,1:T(8,128)(2,1)}), bf16[32,20,2880]{2,0,1:T(8,128)(2,1)}) %reduce-scatter.2.cloned.1.call-update) | async-done | bytes 3686416 | tf_op jit(solution)/shard_map/reduce_scatter | solution.py:215
  668.9 5.3 copy.93
  674.2 8.3 %all-to-all-start.1 = ((bf16[32,20,2880]{2,1,0:T(8,128)(2,1)}), bf16[32,20,2880]{2,1,0:T(8,128)(2,1)}, u32[]{:S(2)}, u32[]{:S(2)}) async-start(bf16[32,20,2880]{2,1,0:T(8,128)(2,1)} %copy.93), calls=%async_computation.2 | async-start | bytes 9043968 | tf_op jit(solution)/shard_map/all_to_all | solution.py:221
  683.1 55.3 %all-to-all-done.1 = bf16[32,20,2880]{2,1,0:T(8,128)(2,1)} async-done(((bf16[32,20,2880]{2,1,0:T(8,128)(2,1)}), bf16[32,20,2880]{2,1,0:T(8,128)(2,1)}, u32[]{:S(2)}, u32[]{:S(2)}) %all-to-all-start.1) | async-done | bytes 3686432 | tf_op jit(solution)/shard_map/all_to_all | solution.py:221
  738.4 6.5 reshape.352
  744.9 9.3 %gather_fusion.1 = bf16[512,2880]{1,0:T(8,128)(2,1)} fusion(bf16[640,2880]{1,0:T(8,128)(2,1)} %reshape.352, s32[1024]{0:T(1024)S(1)} %pad_clamp_fusion), kind=kCustom, calls=%fused_computation.1 | custom fusion | bytes 5900288 | tf_op jit(solution)/shard_map/jit(_take)/gather | solution.py:222
  754.2 5.8 gather.15
  760.0 9.5 %multiply_reduce_fusion = f32[128,2880]{1,0:T(8,128)} fusion(f32[128,4]{1,0:T(8,128)S(1)} %copy.94, bf16[128,4,2880]{2,1,0:T(4,128)(2,1)} %gather.15, pred[128,4]{1,0:T(8,128)(4,1)S(1)} %copy.87), kind=kLoop, calls=%fused_computation.11 | loop fusion | flops 5529600 | bytes 4426240 | tf_op jit(solution)/shard_map/reduce_sum | solution.py:224
  769.5 2.9 copy.95
  772.5 2.8 add_convert_fusion
  (118 shorter events, 36.2 us)
Async XLA Ops:
  6.5 513.8 %copy-start = (bf16[1,384,2880]{1,2,0:T(8,128)(2,1)S(1)}, bf16[1,384,2880]{1,2,0:T(8,128)(2,1)}, u32[]{:S(2)}) copy-start(bf16[1,384,2880]{1,2,0:T(8,128)(2,1)} %param.35) | copy-start | bytes 6635524
  6.5 58.5 %all-gather.8.cloned.1.call-start = ((), (), s32[]{:S(2)}) async-start(), calls=%async_computation.3 | async-start | bytes 5652480 | tf_op jit(solution)/shard_map/all_gather | solution.py:97
  7.3 82.1 %all-gather.12.cloned.1.call-start = ((), (), s32[]{:S(2)}) async-start(), calls=%async_computation.5 | async-start | bytes 1310720 | tf_op jit(solution)/shard_map/all_gather | solution.py:98
  8.0 131.1 %all-gather.10.cloned.1.call-start = ((), (), s32[]{:S(2)}) async-start(), calls=%async_computation.4 | async-start | bytes 2162688 | tf_op jit(solution)/shard_map/all_gather | solution.py:145
  48.1 20.9 %copy-start.6 = (bf16[128,256]{1,0:T(8,128)(2,1)S(1)}, bf16[128,256]{1,0:T(8,128)(2,1)}, u32[]{:S(2)}) copy-start(bf16[128,256]{1,0:T(8,128)(2,1)} %param.21) | copy-start | bytes 196612
  48.1 22.0 %copy-start.5 = (bf16[128,256]{1,0:T(8,128)(2,1)S(1)}, bf16[128,256]{1,0:T(8,128)(2,1)}, u32[]{:S(2)}) copy-start(bf16[128,256]{1,0:T(8,128)(2,1)} %param.22) | copy-start | bytes 196612
  48.1 24.1 %copy-start.9 = (s32[128,4]{0,1:T(4,128)S(1)}, s32[128,4]{0,1:T(4,128)}, u32[]{:S(2)}) copy-start(s32[128,4]{0,1:T(4,128)} %param.36) | copy-start | bytes 6148
  48.1 24.4 %copy-start.14 = (s32[1,128]{1,0:T(1,128)S(1)}, s32[1,128]{1,0:T(1,128)}, u32[]{:S(2)}) copy-start(s32[1,128]{1,0:T(1,128)} %param.23) | copy-start | bytes 1540
  48.2 26.3 %copy-start.16 = (f32[32]{0:T(128)S(1)}, f32[32]{0:T(128)}, u32[]{:S(2)}) copy-start(f32[32]{0:T(128)} %param.25) | copy-start | bytes 388
  48.2 41.2 %copy-start.4 = (bf16[128,2048]{1,0:T(8,128)(2,1)S(1)}, bf16[128,2048]{1,0:T(8,128)(2,1)}, u32[]{:S(2)}) copy-start(bf16[128,2048]{1,0:T(8,128)(2,1)} %param.20) | copy-start | bytes 1572868
  70.1 116.4 %all-gather.14.cloned.1.call-start = ((), (), s32[]{:S(2)}) async-start(), calls=%async_computation.6 | async-start | bytes 2162688 | tf_op jit(solution)/shard_map/all_gather | solution.py:146
  71.0 145.3 %all-gather.16.cloned.1.call-start = ((), (), s32[]{:S(2)}) async-start(), calls=%async_computation.7 | async-start | bytes 1310720 | tf_op jit(solution)/shard_map/all_gather | solution.py:100
  71.6 164.8 %all-gather.18.cloned.1.call-start = ((), (), s32[]{:S(2)}) async-start(), calls=%async_computation.8 | async-start | bytes 1884160 | tf_op jit(solution)/shard_map/all_gather | solution.py:101
  72.1 384.7 %all-gather.20.cloned.1.call-start = ((), (), s32[]{:S(2)}) async-start(), calls=%async_computation.9 | async-start | bytes 18841600 | tf_op jit(solution)/shard_map/all_gather | solution.py:208
  76.3 88.1 %copy-start.7 = (s32[512]{0:T(512)}, s32[512]{0:T(512)S(1)}, u32[]{:S(2)}) copy-start(s32[512]{0:T(512)S(1)} %fusion.48) | copy-start | bytes 6148
  76.3 0.6 copy-start.12
  216.2 0.8 copy-start.17
  218.7 17.6 %copy-start.3 = (bf16[128,2880]{0,1:T(8,128)(2,1)S(1)}, bf16[128,2880]{0,1:T(8,128)(2,1)}, u32[]{:S(2)}) copy-start(bf16[128,2880]{0,1:T(8,128)(2,1)} %param.19) | copy-start | bytes 2211844
  228.0 12.1 %copy-start.11 = (f32[2880]{0:T(1024)S(1)}, f32[2880]{0:T(1024)}, u32[]{:S(2)}) copy-start(f32[2880]{0:T(1024)} %param.33) | copy-start | bytes 34564
  239.0 1.1 copy-start.2
  321.2 347.7 %reduce-scatter.2.cloned.1.call-start = ((), (), s32[]{:S(2)}) async-start(), calls=%async_computation.10 | async-start | bytes 18841600 | tf_op jit(solution)/shard_map/reduce_scatter | solution.py:215
  472.8 33.8 %slice-start = ((s8[4423680]{0:T(1024)(128)(4,1)}), s8[229376]{0:T(1024)(128)(4,1)S(1)}, s32[]{:S(2)}) async-start(s8[4423680]{0:T(1024)(128)(4,1)} %bitcast.138), calls=%async_computation.11 | async-start | bytes 458752
  494.1 12.6 %copy-start.1 = (bf16[2560,2880]{1,0:T(8,128)(2,1)S(1)}, bf16[2560,2880]{1,0:T(8,128)(2,1)}, u32[]{:S(2)}) copy-start(bf16[2560,2880]{1,0:T(8,128)(2,1)} %reshape_squeeze_reshape.3) | copy-start | bytes 44236804
  494.1 12.6 %slice-start.1 = ((s8[4423680]{0:T(1024)(128)(4,1)}), s8[4194304]{0:T(1024)(128)(4,1)S(1)}, s32[]{:S(2)}) async-start(s8[4423680]{0:T(1024)(128)(4,1)} %bitcast.138), calls=%async_computation.12 | async-start | bytes 8388608
  674.2 8.4 %copy-start.8 = (s32[512]{0:T(512)S(1)}, s32[512]{0:T(512)}, u32[]{:S(2)}) copy-start(s32[512]{0:T(512)} %copy-done.7) | copy-start | bytes 6148
  674.2 8.5 %copy-start.10 = (s32[128,4]{0,1:T(4,128)S(1)}, s32[128,4]{0,1:T(4,128)}, u32[]{:S(2)}) copy-start(s32[128,4]{0,1:T(4,128)} %param.36) | copy-start | bytes 6148
  674.2 8.7 %copy-start.15 = (f32[128,4]{0,1:T(4,128)S(1)}, f32[128,4]{0,1:T(4,128)}, u32[]{:S(2)}) copy-start(f32[128,4]{0,1:T(4,128)} %param.37) | copy-start | bytes 6148
  674.2 8.8 %copy-start.13 = (s32[512,1]{0,1:T(1,128)S(1)}, s32[512,1]{0,1:T(1,128)}, u32[]{:S(2)}) copy-start(s32[512,1]{0,1:T(1,128)} %copy-done.12) | copy-start | bytes 6148
  674.2 64.2 %all-to-all-start.1 = ((bf16[32,20,2880]{2,1,0:T(8,128)(2,1)}), bf16[32,20,2880]{2,1,0:T(8,128)(2,1)}, u32[]{:S(2)}, u32[]{:S(2)}) async-start(bf16[32,20,2880]{2,1,0:T(8,128)(2,1)} %copy.93), calls=%async_computation.2 | async-start | bytes 9043968 | tf_op jit(solution)/shard_map/all_to_all | solution.py:221
Sparse Core Ops, SparseCore 0:
  9.0 56.0 all-gather.7
  66.7 22.5 all-gather.11
  91.5 47.5 all-gather.9
  141.2 43.0 all-gather.13
  185.8 20.8 all-gather.15
  208.2 28.1 all-gather.17
  321.3 135.4 all-gather.19
  533.1 135.7 reduce-scatter.1
where the time goes:
time: 790 us; the launch traced here: 782 us
  waiting for transfers between devices  407 us (52%)
  matrix products  107 us (14%)
  local copies, waits for them, and re-layouts  99.5 us (13%)
  blocking collectives  99.4 us (13%)
  other arithmetic  46.5 us (6%)
  between operations  14.2 us (2%)
  starting transfers between devices  8.63 us (1%)
    reduce_scatter x1, waiting for transfers between devices, shards(): lax.psum_scatter(jnp.stack(outputs, axis=1).reshape(row_count, item_count...  136 us
    all_gather x1, waiting for transfers between devices, shards(): gathered = lax.all_gather(arrived, 'dp', axis=0, tiled=True)  136 us
    all_to_all x1, blocking collectives, shards(): lax.all_to_all(dispatch, 'expert', split_axis=0, concat_axis=0, tiled=True)  62.3 us
    all_to_all x1, waiting for transfers between devices, shards(): lax.all_to_all(summed, 'expert', split_axis=0, concat_axis=0, tiled=True)  55.3 us
    all_gather x1, waiting for transfers between devices, shards(): piece_keys = lax.all_gather(key_rows, 'expert', axis=0, tiled=True)  43.3 us
    dot_general x4, matrix products, multiply_rows(): lax.dot_general(left, right, (((1,), (1,)), ((), ())), preferred_element_...  27.9 us
    dot_general x1, matrix products, shards(): jnp.einsum('kgtn,nkd->kgtd', exps.astype(jnp.bfloat16), piece_values, pre...  25.5 us
    dot_general x1, matrix products, shards(): jnp.einsum('tkgd,nkd->kgtn', queries, piece_keys, preferred_element_type=...  25.3 us
  transfers between devices with their start and end apart: 9, of which 7 were waited for; matrix products, arithmetic and copies ran while one was open for 14% of the time, Pallas kernels for 0%

commit v1 on v0

--- a/solution.py
+++ b/solution.py
@@ -93,13 +93,24 @@
     query_index = lax.axis_index("expert") * tok_rows + jnp.arange(tok_rows, dtype=jnp.int32)
     positions = query_index - jnp.sum(doc_hot * firsts[None, :], axis=1)
     adapter_of = jnp.sum(doc_hot * prompt_adapter[0][None, :], axis=1)
-    factors = (
-        lax.all_gather(adapter_down_factors, "dp", axis=0, tiled=True),
-        lax.all_gather(query_up_factors, "dp", axis=0, tiled=True),
-        lax.all_gather(key_value_up_factors, "dp", axis=0, tiled=True),
-        lax.all_gather(output_down_factors, "dp", axis=0, tiled=True),
-        lax.all_gather(output_up_factors, "dp", axis=0, tiled=True),
-    )
+    local_factors = (
+        adapter_down_factors,
+        query_up_factors,
+        key_value_up_factors,
+        output_down_factors,
+        output_up_factors,
+    )
+    local_count = adapter_down_factors.shape[0]
+    joined_factors = jnp.concatenate([f.reshape(local_count, -1) for f in local_factors], axis=1)
+    all_factors = lax.all_gather(joined_factors, "dp", axis=0, tiled=True)
+    factors = []
+    offset = 0
+    for f in local_factors:
+        width = f.shape[1] * f.shape[2]
+        factors.append(
+            all_factors[:, offset : offset + width].reshape(all_factors.shape[0], f.shape[1], f.shape[2])
+        )
+        offset += width
     all_down, all_up_query, all_up_keyval, all_o_down, all_o_up = factors
     adapter_table = all_down.shape[0]
     adapter_selector = (
@@ -142,11 +153,18 @@
     running_max = jnp.broadcast_to(sink_grid[:, :, None], (kv_heads, groups, tok_rows))
     running_sum = jnp.ones((kv_heads, groups, tok_rows), jnp.float32)
     weighted = jnp.zeros((kv_heads, groups, tok_rows, HD), jnp.float32)
-    piece_keys = lax.all_gather(key_rows, "expert", axis=0, tiled=True)
-    piece_values = lax.all_gather(value_rows, "expert", axis=0, tiled=True)
-    piece_rows = piece_keys.shape[0]
-    piece_keys = piece_keys.reshape(piece_rows, kv_heads, HD)
-    piece_values = piece_values.reshape(piece_rows, kv_heads, HD)
+    piece_kv = lax.all_gather(
+        jnp.concatenate([key_rows, value_rows], axis=1), "expert", axis=0, tiled=True
+    )
+    piece_rows = piece_kv.shape[0]
+    piece_keys = piece_kv[:, :kv_width].reshape(piece_rows, kv_heads, HD)
+    piece_values = piece_kv[:, kv_width:].reshape(piece_rows, kv_heads, HD)
+    gate_up_local = jnp.transpose(expert_gate_up_weight[0], (1, 0, 2))
+    gate_up_local, down_local, _ = lax.optimization_barrier(
+        (gate_up_local, expert_down_weight[0], piece_kv)
+    )
+    gate_up_full = lax.all_gather(gate_up_local, "dp", axis=1, tiled=True)
+    down_full = lax.all_gather(down_local, "dp", axis=0, tiled=True)
     key_index = jnp.arange(piece_rows, dtype=jnp.int32)
     scores = (
         jnp.einsum("tkgd,nkd->kgtn", queries, piece_keys, preferred_element_type=jnp.float32)
@@ -203,22 +221,22 @@
         experts, capacity, model_width
     )
     arrived = lax.all_to_all(dispatch, "expert", split_axis=0, concat_axis=0, tiled=True)
-    sender_rows = arrived.shape[0]
-    item_count = arrived.shape[1]
-    gathered = lax.all_gather(arrived, "dp", axis=0, tiled=True)
-    row_count = sender_rows * lax.axis_size("dp")
-    grouped = gathered.reshape(row_count // exp_dev, exp_dev, item_count, model_width)
-    flat_rows = grouped[:, 0].reshape(-1, model_width)
-    activation = expert_hidden(flat_rows, expert_gate_up_weight[0])
-    product = jnp.dot(activation, expert_down_weight[0], preferred_element_type=jnp.float32)
-    outputs = [product.reshape(row_count // exp_dev, item_count, model_width)]
-    summed = lax.psum_scatter(
-        jnp.stack(outputs, axis=1).reshape(row_count, item_count, model_width).astype(jnp.bfloat16),
-        "dp",
-        scatter_dimension=0,
-        tiled=True,
-    )
-    returned = lax.all_to_all(summed, "expert", split_axis=0, concat_axis=0, tiled=True)
+    flat_rows = arrived.reshape(-1, model_width)
+    gate_out = multiply_rows(flat_rows, gate_up_full[0])
+    up_out = multiply_rows(flat_rows, gate_up_full[1])
+    activation = (jax.nn.silu(gate_out) * up_out).astype(jnp.bfloat16)
+    block_units = expert_gate_up_weight.shape[1]
+    block_count = down_full.shape[0] // block_units
+    summed = jnp.zeros((flat_rows.shape[0], model_width), jnp.float32)
+    for quarter in range(block_count):
+        part = jnp.dot(
+            activation[:, quarter * block_units : (quarter + 1) * block_units],
+            down_full[quarter * block_units : (quarter + 1) * block_units],
+            preferred_element_type=jnp.float32,
+        )
+        summed = summed + part.astype(jnp.bfloat16).astype(jnp.float32)
+    expert_rows = summed.astype(jnp.bfloat16).reshape(arrived.shape)
+    returned = lax.all_to_all(expert_rows, "expert", split_axis=0, concat_axis=0, tiled=True)
     chosen = jnp.take(returned.reshape(experts * capacity, model_width), buffer_index, axis=0)
     scaled = chosen.astype(jnp.float32) * routing_gate_weight.reshape(tok_rows * TOP)[:, None]
     moe = jnp.sum(scaled.reshape(tok_rows, TOP, model_width), axis=1)

time: 790 us -> 570 us (0.72)
  waiting for transfers between devices: 407 us -> 204 us
  blocking collectives: 99.4 us -> 84.5 us
  matrix products: 107 us -> 96.5 us
  local copies, waits for them, and re-layouts: 99.5 us -> 109 us
    reduce_scatter x1 -> x0, waiting for transfers between devices: 136 us -> none  [shards(): lax.psum_scatter(jnp.stack(outputs, axis=1).reshape(row_count, item_count...]
    all_gather x7 -> x4, waiting for transfers between devices: 214 us -> 148 us  [the longest x1 59.6 us: shards(): all_factors = lax.all_gather(joined_factors, 'dp', axis=0, tiled=True)]
    all_gather x2 -> x0, local copies, waits for them, and re-layouts: 20.1 us -> none  [the longest x1 16 us: shards(): gathered = lax.all_gather(arrived, 'dp', axis=0, tiled=True)]
    another operation x3 -> x4, local copies, waits for them, and re-layouts: 21.3 us -> 2.84 us  [the longest x1 2.24 us: shards(): all_o_up.reshape(adapter_table * ADAPTER_RANK, model_width)]
    unnamed x42 -> x69, local copies, waits for them, and re-layouts: 2.74 us -> 20 us
    slice x1 -> x10, local copies, waits for them, and re-layouts: 0.22 us -> 16.7 us  [the longest x2 6.92 us: shards(): piece_keys = piece_kv[:, :kv_width].reshape(piece_rows, kv_heads, HD)]
    reshape x0 -> x4, local copies, waits for them, and re-layouts: none -> 14.8 us  [the longest x1 6.53 us: shards(): flat_rows = arrived.reshape(-1, model_width)]
    all_gather x1 -> x0, blocking collectives: 12.8 us -> none  [shards(): lax.all_gather(key_value_up_factors, 'dp', axis=0, tiled=True)]
  transfers between devices with their start and end apart: 9 -> 5, of which waited for: 7 -> 4; matrix products, arithmetic and copies ran while one was open for 14% -> 27% of each run, Pallas kernels for 0% -> 0%
where the time goes in v1:
time: 570 us; the launch traced here: 559 us
  waiting for transfers between devices  204 us (36%)
  local copies, waits for them, and re-layouts  109 us (19%)
  matrix products  96.5 us (17%)
  blocking collectives  84.5 us (15%)
  other arithmetic  43.3 us (8%)
  between operations  14 us (2%)
  starting transfers between devices  8.53 us (1%)
    all_to_all x1, blocking collectives, shards(): lax.all_to_all(dispatch, 'expert', split_axis=0, concat_axis=0, tiled=True)  60.1 us
    all_gather x1, waiting for transfers between devices, shards(): all_factors = lax.all_gather(joined_factors, 'dp', axis=0, tiled=True)  59.6 us
    all_to_all x1, waiting for transfers between devices, shards(): lax.all_to_all(expert_rows, 'expert', split_axis=0, concat_axis=0, tiled=...  55.3 us
    all_gather x1, waiting for transfers between devices, shards(): lax.all_gather(jnp.concatenate([key_rows, value_rows], axis=1), 'expert',...  47.8 us
    all_gather x1, waiting for transfers between devices, shards(): down_full = lax.all_gather(down_local, 'dp', axis=0, tiled=True)  40.7 us
    dot_general x1, matrix products, shards(): jnp.einsum('kgtn,nkd->kgtd', exps.astype(jnp.bfloat16), piece_values, pre...  24.7 us
    all_gather x1, blocking collectives, shards(): row_ids = lax.all_gather(prompt_number, 'expert', axis=1, tiled=True)[0]  24.3 us
    dot_general x1, matrix products, shards(): jnp.einsum('tkgd,nkd->kgtn', queries, piece_keys, preferred_element_type=...  23.8 us
  transfers between devices with their start and end apart: 5, of which 4 were waited for; matrix products, arithmetic and copies ran while one was open for 27% of the time, Pallas kernels for 0%

profile of v1, /device:TPU:1, one launch (start us, length us, event | category | flops | bytes accessed | tf_op | source)
XLA Modules:
  0.0 559.3 jit_solution(11640348765024524494)
XLA Ops:
  17.2 24.3 %all_gather.17 = s32[1,4096]{1,0:T(1,128)S(1)} all-gather(s32[1,128]{1,0:T(1,128)S(1)} %copy-done.18), channel_id=1, replica_groups=mesh['dp'=4,'expert'=32] {'expert'}, dimensions={1}, use_global_device_ids=true | all-gather | bytes 16896 | tf_op jit(solution)/shard_map/all_gather | solution.py:87
  42.6 59.6 %all-gather.12.cloned.1.call-done = bf16[4,4,258048]{2,1,0:T(4,128)(2,1)} async-done(((bf16[1,4,258048]{2,1,0:T(4,128)(2,1)}), bf16[4,4,258048]{2,1,0:T(4,128)(2,1)}) %all-gather.12.cloned.1.call-update) | async-done | bytes 8257552 | tf_op jit(solution)/shard_map/all_gather | solution.py:105
  102.2 6.4 %reshape.424 = bf16[16,258048]{1,0:T(8,128)(2,1)} reshape(bf16[4,4,258048]{2,1,0:T(4,128)(2,1)} %all-gather.12.cloned.1.call-done) | data formatting | bytes 16515072
  108.6 3.9 slice.116
  112.6 6.7 %dot_general.51 = bf16[16,48,2880]{2,1,0:T(8,128)(2,1)} reshape(bf16[16,138240]{1,0:T(8,128)(2,1)} %slice.116) | data formatting | bytes 8847360 | tf_op jit(solution)/shard_map/dot_general | solution.py:38
  119.3 3.8 fusion.31
  124.6 47.8 %all-gather.6.cloned.1.call-done = bf16[4096,512]{1,0:T(8,128)(2,1)} async-done(((bf16[128,512]{1,0:T(8,128)(2,1)}), bf16[4096,512]{1,0:T(8,128)(2,1)}) %all-gather.6.cloned.1.call-update) | async-done | bytes 4194320 | tf_op jit(solution)/shard_map/all_gather | solution.py:156
  193.7 4.0 fusion.66
  197.7 3.0 copy.83
  203.6 23.8 %fusion.2 = (f32[4,8,128]{2,1,0:T(8,128)S(1)}, f32[4,4096,128,8]{2,1,3,0:T(8,128)}) fusion(pred[128,4096]{0,1:T(8,128)(4,1)S(1)} %fusion.15, bf16[4096,4,64,1]{0,2,3,1:T(8,128)(2,1)S(1)} %bitcast.124, bf16[128,4,8,32]{0,3,2,1:T(8,128)(2,1)S(1)} %bitcast.132, bf16[128,4,8,32]{0,3,2,1:T(8,128)(2,1)S(1)} %bitcast.131), kind=kOutput, calls=%fused_computation.7 | convolution fusion | flops 2198859776 | bytes 70270976 | tf_op jit(solution)/shard_map/tkgd,nkd->kgtn/dot_general | solution.py:170
  227.4 22.3 %fusion = f32[4,8,128]{2,1,0:T(8,128)S(1)} fusion(f32[4,4096,128,8]{2,1,3,0:T(8,128)} %get-tuple-element.30, f32[4,8,128]{2,1,0:T(8,128)S(1)} %broadcast_maximum_fusion, pred[128,4096]{0,1:T(8,128)(4,1)S(1)} %fusion.15), kind=kLoop, calls=%fused_computation.5 | loop fusion | flops 67104768 | bytes 67665920 | tf_op jit(solution)/shard_map/reduce_sum | solution.py:178
  249.8 24.7 %fusion.28 = bf16[128,4,8,64]{0,3,2,1:T(8,128)(2,1)S(1)} fusion(bf16[4096,4,64,1]{0,2,3,1:T(8,128)(2,1)S(1)} %bitcast.130, f32[4,4096,128,8]{2,1,3,0:T(8,128)} %get-tuple-element.30, f32[4,8,128]{2,1,0:T(8,128)S(1)} %broadcast_maximum_fusion, pred[128,4096]{0,1:T(8,128)(4,1)S(1)} %fusion.15, f32[128,4,8]{0,2,1:T(8,128)S(1)} %get-tuple-element.22, ...), kind=kOutput, calls=%fused_computation.44 | convolution fusion | flops 2215378944 | bytes 70303744 | tf_op jit(solution)/shard_map/kgtn,nkd->kgtd/dot_general | solution.py:179
  275.0 6.7 %fusion.67 = f32[128,2880]{0,1:T(8,128)S(1)} fusion(bf16[2048,2880]{0,1:T(8,128)(2,1)} %param.32, bf16[128,2048]{0,1:T(8,128)(2,1)S(1)} %bitcast.158), kind=kOutput, calls=%fused_computation.137 | convolution fusion | flops 1509949440 | bytes 13795328 | tf_op jit(solution)/shard_map/dot_general | solution.py:195
  283.4 4.6 gather_fusion
  288.0 6.5 %gather.13 = bf16[32,20,2880]{2,1,0:T(8,128)(2,1)} reshape(bf16[640,2880]{1,0:T(8,128)(2,1)} %gather_fusion) | data formatting | bytes 7372800 | tf_op jit(solution)/shard_map/jit(_take)/gather | solution.py:219
  297.3 60.1 %all_to_all.10 = bf16[32,20,2880]{2,1,0:T(8,128)(2,1)} all-to-all(bf16[32,20,2880]{2,1,0:T(8,128)(2,1)S(1)} %select_select_fusion), channel_id=1, replica_groups=mesh['dp'=4,'expert'=32] {'expert'}, dimensions={0} | all-to-all | bytes 7372800 | tf_op jit(solution)/shard_map/all_to_all | solution.py:223
  357.4 6.5 %reshape.395 = bf16[640,2880]{1,0:T(8,128)(2,1)} reshape(bf16[32,20,2880]{2,1,0:T(8,128)(2,1)} %all_to_all.10) | data formatting | bytes 7372800 | tf_op jit(solution)/shard_map/reshape | solution.py:224
  363.9 10.0 %fusion.7 = f32[640,1536]{1,0:T(8,128)S(1)} fusion(bf16[640,2880]{1,0:T(8,128)(2,1)} %reshape.395, bf16[2,1536,2880]{1,2,0:T(8,128)(2,1)} %all-gather.8.cloned.1.call-done), kind=kOutput, calls=%fused_computation.13 | convolution fusion | flops 5662310400 | bytes 16547840 | tf_op jit(solution)/shard_map/dot_general | solution.py:38
  375.1 8.1 %multiply_convert_fusion = bf16[640,1536]{1,0:T(8,128)(2,1)} fusion(f32[640,1536]{1,0:T(8,128)S(1)} %fusion.7, bf16[640,2880]{1,0:T(8,128)(2,1)S(1)} %copy-done.2, bf16[2,1536,2880]{1,2,0:T(8,128)(2,1)S(1)} %copy-done.22), kind=kOutput, calls=%fused_computation.21 | convolution fusion | flops 5668208640 | bytes 18513920 | tf_op jit(solution)/shard_map/dot_general | solution.py:38
  383.2 40.7 %all-gather.10.cloned.1.call-done = bf16[1536,2880]{0,1:T(8,128)(2,1)} async-done(((bf16[384,2880]{0,1:T(8,128)(2,1)}), bf16[1536,2880]{0,1:T(8,128)(2,1)}) %all-gather.10.cloned.1.call-update) | async-done | bytes 8847376 | tf_op jit(solution)/shard_map/all_gather | solution.py:167
  423.9 4.2 convolution_convert_fusion
  428.1 4.2 convolution_convert_fusion.1
  434.7 4.5 add_convert_fusion
  439.2 6.2 %copy.93 = bf16[640,2880]{1,0:T(8,128)(2,1)} copy(bf16[640,2880]{0,1:T(8,128)(2,1)} %add_convert_fusion) | data formatting | bytes 7372800 | tf_op jit(solution)/shard_map/convert_element_type | solution.py:238
  445.4 6.5 %reshape.396 = bf16[32,20,2880]{2,1,0:T(8,128)(2,1)} reshape(bf16[640,2880]{1,0:T(8,128)(2,1)} %copy.93) | data formatting | bytes 7372800 | tf_op jit(solution)/shard_map/reshape | solution.py:238
  451.9 8.4 %all-to-all-start.1 = ((bf16[32,20,2880]{2,1,0:T(8,128)(2,1)}), bf16[32,20,2880]{2,1,0:T(8,128)(2,1)}, u32[]{:S(2)}, u32[]{:S(2)}) async-start(bf16[32,20,2880]{2,1,0:T(8,128)(2,1)} %reshape.396), calls=%async_computation.1 | async-start | bytes 9043968 | tf_op jit(solution)/shard_map/all_to_all | solution.py:239
  460.8 55.3 %all-to-all-done.1 = bf16[32,20,2880]{2,1,0:T(8,128)(2,1)} async-done(((bf16[32,20,2880]{2,1,0:T(8,128)(2,1)}), bf16[32,20,2880]{2,1,0:T(8,128)(2,1)}, u32[]{:S(2)}, u32[]{:S(2)}) %all-to-all-start.1) | async-done | bytes 3686432 | tf_op jit(solution)/shard_map/all_to_all | solution.py:239
  516.1 6.5 %reshape.397 = bf16[640,2880]{1,0:T(8,128)(2,1)} reshape(bf16[32,20,2880]{2,1,0:T(8,128)(2,1)} %all-to-all-done.1) | data formatting | bytes 7372800 | tf_op jit(solution)/shard_map/reshape | solution.py:240
  522.6 9.3 %gather_fusion.1 = bf16[512,2880]{1,0:T(8,128)(2,1)} fusion(bf16[640,2880]{1,0:T(8,128)(2,1)} %reshape.397, s32[1024]{0:T(1024)S(1)} %pad_clamp_fusion), kind=kCustom, calls=%fused_computation.1 | custom fusion | bytes 5900288 | tf_op jit(solution)/shard_map/jit(_take)/gather | solution.py:240
  531.9 5.8 %gather.15 = bf16[128,4,2880]{2,1,0:T(4,128)(2,1)} reshape(bf16[512,2880]{1,0:T(8,128)(2,1)} %gather_fusion.1) | data formatting | bytes 5898240 | tf_op jit(solution)/shard_map/jit(_take)/gather | solution.py:240
  537.7 9.5 %multiply_reduce_fusion = f32[128,2880]{1,0:T(8,128)} fusion(f32[128,4]{1,0:T(8,128)S(1)} %copy.94, bf16[128,4,2880]{2,1,0:T(4,128)(2,1)} %gather.15, pred[128,4]{1,0:T(8,128)(4,1)S(1)} %copy.90), kind=kLoop, calls=%fused_computation.15 | loop fusion | flops 5529600 | bytes 4426240 | tf_op jit(solution)/shard_map/reduce_sum | solution.py:242
  547.2 3.0 copy.95
  (151 shorter events, 48.4 us)
Async XLA Ops:
  6.5 3.5 copy-start.8
  6.5 95.7 %all-gather.12.cloned.1.call-start = ((), (), s32[]{:S(2)}) async-start(), calls=%async_computation.5 | async-start | bytes 10321920 | tf_op jit(solution)/shard_map/all_gather | solution.py:105
  9.5 7.6 %copy-start.18 = (s32[1,128]{1,0:T(1,128)S(1)}, s32[1,128]{1,0:T(1,128)}, u32[]{:S(2)}) copy-start(s32[1,128]{1,0:T(1,128)} %param.23) | copy-start | bytes 1540
  9.5 32.4 %copy-start.20 = (s32[1,16]{1,0:T(1,128)S(1)}, s32[1,16]{1,0:T(1,128)}, u32[]{:S(2)}) copy-start(s32[1,16]{1,0:T(1,128)} %param.24) | copy-start | bytes 196
  10.0 32.0 %copy-start.3 = (bf16[128,2880]{0,1:T(8,128)(2,1)S(1)}, bf16[128,2880]{0,1:T(8,128)(2,1)}, u32[]{:S(2)}) copy-start(bf16[128,2880]{0,1:T(8,128)(2,1)} %param.19) | copy-start | bytes 2211844
  17.1 155.3 %all-gather.6.cloned.1.call-start = ((), (), s32[]{:S(2)}) async-start(), calls=%async_computation.2 | async-start | bytes 4325376 | tf_op jit(solution)/shard_map/all_gather | solution.py:156
  108.6 3.9 slice-start
  112.6 6.7 %copy-start.23 = (f32[2880]{0:T(1024)S(1)}, f32[2880]{0:T(1024)}, u32[]{:S(2)}) copy-start(f32[2880]{0:T(1024)} %param.26) | copy-start | bytes 34564
  119.3 3.8 copy-start.10
  119.3 4.3 copy-start.9
  123.1 49.4 %copy-start.13 = (s32[128,4]{0,1:T(4,128)S(1)}, s32[128,4]{0,1:T(4,128)}, u32[]{:S(2)}) copy-start(s32[128,4]{0,1:T(4,128)} %param.36) | copy-start | bytes 6148
  123.1 49.7 %copy-start.21 = (f32[32]{0:T(128)S(1)}, f32[32]{0:T(128)}, u32[]{:S(2)}) copy-start(f32[32]{0:T(128)} %param.25) | copy-start | bytes 388
  124.5 239.4 %all-gather.8.cloned.1.call-start = ((), (), s32[]{:S(2)}) async-start(), calls=%async_computation.3 | async-start | bytes 22118400 | tf_op jit(solution)/shard_map/all_gather | solution.py:166
  172.4 251.5 %all-gather.10.cloned.1.call-start = ((), (), s32[]{:S(2)}) async-start(), calls=%async_computation.4 | async-start | bytes 11059200 | tf_op jit(solution)/shard_map/all_gather | solution.py:167
  174.7 8.1 %copy-start.11 = (s32[512]{0:T(512)}, s32[512]{0:T(512)S(1)}, u32[]{:S(2)}) copy-start(s32[512]{0:T(512)S(1)} %fusion.52) | copy-start | bytes 6148
  183.3 7.3 %slice-start.1 = ((bf16[16,258048]{1,0:T(8,128)(2,1)}), bf16[16,46080]{1,0:T(8,128)(2,1)S(1)}, s32[]{:S(2)}) async-start(bf16[16,258048]{1,0:T(8,128)(2,1)} %reshape.424), calls=%async_computation.7 | async-start | bytes 2949120 | tf_op jit(solution)/shard_map/slice | solution.py:111
  197.7 5.9 %copy-start.6 = (bf16[128,32,32]{0,2,1:T(8,128)(2,1)S(1)}, bf16[128,32,32]{0,2,1:T(8,128)(2,1)}, u32[]{:S(2)}) copy-start(bf16[128,32,32]{0,2,1:T(8,128)(2,1)} %get-tuple-element.18) | copy-start | bytes 786436
  227.4 22.4 %copy-start.5 = (bf16[4096,256]{0,1:T(8,128)(2,1)S(1)}, bf16[4096,256]{0,1:T(8,128)(2,1)}, u32[]{:S(2)}) copy-start(bf16[4096,256]{0,1:T(8,128)(2,1)} %copy.83) | copy-start | bytes 6291460
  249.8 24.7 %copy-start.7 = (bf16[2,8,16,2048]{3,2,1,0:T(8,128)(2,1)S(1)}, bf16[2,8,16,2048]{3,2,1,0:T(8,128)(2,1)}, u32[]{:S(2)}) copy-start(bf16[2,8,16,2048]{3,2,1,0:T(8,128)(2,1)} %copy.106) | copy-start | bytes 3145732
  275.0 6.7 %copy-start = (bf16[256,2880]{1,0:T(8,128)(2,1)S(1)}, bf16[256,2880]{1,0:T(8,128)(2,1)}, u32[]{:S(2)}) copy-start(bf16[256,2880]{1,0:T(8,128)(2,1)} %reshape_reshape.9) | copy-start | bytes 4423684
  275.0 6.7 %copy-start.4 = (bf16[128,2880]{0,1:T(8,128)(2,1)S(1)}, bf16[128,2880]{0,1:T(8,128)(2,1)}, u32[]{:S(2)}) copy-start(bf16[128,2880]{0,1:T(8,128)(2,1)} %param.19) | copy-start | bytes 2211844
  363.9 10.1 %copy-start.2 = (bf16[640,2880]{1,0:T(8,128)(2,1)S(1)}, bf16[640,2880]{1,0:T(8,128)(2,1)}, u32[]{:S(2)}) copy-start(bf16[640,2880]{1,0:T(8,128)(2,1)} %reshape.395) | copy-start | bytes 11059204
  363.9 11.2 %copy-start.22 = (bf16[2,1536,2880]{1,2,0:T(8,128)(2,1)S(1)}, bf16[2,1536,2880]{1,2,0:T(8,128)(2,1)}, u32[]{:S(2)}) copy-start(bf16[2,1536,2880]{1,2,0:T(8,128)(2,1)} %all-gather.8.cloned.1.call-done) | copy-start | bytes 53084164
  423.9 8.5 %slice-start.2 = ((s8[8847360]{0:T(1024)(128)(4,1)}), s8[4194304]{0:T(1024)(128)(4,1)S(1)}, s32[]{:S(2)}) async-start(s8[8847360]{0:T(1024)(128)(4,1)} %bitcast.155), calls=%async_computation.8 | async-start | bytes 8388608
  423.9 8.5 %slice-start.3 = ((s8[8847360]{0:T(1024)(128)(4,1)}), s8[4194304]{0:T(1024)(128)(4,1)S(1)}, s32[]{:S(2)}) async-start(s8[8847360]{0:T(1024)(128)(4,1)} %bitcast.155), calls=%async_computation.9 | async-start | bytes 8388608
  428.1 4.3 slice-start.4
  428.1 4.3 copy-start.24
  451.9 8.4 %copy-start.12 = (s32[512]{0:T(512)S(1)}, s32[512]{0:T(512)}, u32[]{:S(2)}) copy-start(s32[512]{0:T(512)} %copy-done.11) | copy-start | bytes 6148
  451.9 8.5 %copy-start.19 = (f32[128,4]{0,1:T(4,128)S(1)}, f32[128,4]{0,1:T(4,128)}, u32[]{:S(2)}) copy-start(f32[128,4]{0,1:T(4,128)} %param.37) | copy-start | bytes 6148
  451.9 8.7 %copy-start.14 = (s32[128,4]{0,1:T(4,128)S(1)}, s32[128,4]{0,1:T(4,128)}, u32[]{:S(2)}) copy-start(s32[128,4]{0,1:T(4,128)} %param.36) | copy-start | bytes 6148
  451.9 8.9 %copy-start.17 = (s32[512,1]{0,1:T(1,128)S(1)}, s32[512,1]{0,1:T(1,128)}, u32[]{:S(2)}) copy-start(s32[512,1]{0,1:T(1,128)} %copy-done.16) | copy-start | bytes 6148
  451.9 64.2 %all-to-all-start.1 = ((bf16[32,20,2880]{2,1,0:T(8,128)(2,1)}), bf16[32,20,2880]{2,1,0:T(8,128)(2,1)}, u32[]{:S(2)}, u32[]{:S(2)}) async-start(bf16[32,20,2880]{2,1,0:T(8,128)(2,1)} %reshape.396), calls=%async_computation.1 | async-start | bytes 9043968 | tf_op jit(solution)/shard_map/all_to_all | solution.py:239
  (3 other events, 2.8 us)
Sparse Core Ops, SparseCore 0:
  17.2 84.9 all-gather.11
  124.6 47.7 all-gather.5
  174.1 161.4 all-gather.7
  337.1 86.7 all-gather.9

commit v2 on v1

--- a/solution.py
+++ b/solution.py
@@ -165,12 +165,21 @@
     )
     gate_up_full = lax.all_gather(gate_up_local, "dp", axis=1, tiled=True)
     down_full = lax.all_gather(down_local, "dp", axis=0, tiled=True)
-    key_index = jnp.arange(piece_rows, dtype=jnp.int32)
+    window = min(piece_rows, piece_rows // 2 + tok_rows)
+    window_start = jnp.clip(
+        (lax.axis_index("expert") + 1) * tok_rows - window, 0, piece_rows - window
+    )
+    piece_keys = lax.dynamic_slice_in_dim(piece_keys, window_start, window, 0)
+    piece_values = lax.dynamic_slice_in_dim(piece_values, window_start, window, 0)
+    window_ids = lax.dynamic_slice_in_dim(row_ids, window_start, window, 0)
+    key_index = window_start + jnp.arange(window, dtype=jnp.int32)
     scores = (
         jnp.einsum("tkgd,nkd->kgtn", queries, piece_keys, preferred_element_type=jnp.float32)
         * SCORE_SCALE
     )
-    allowed = (key_index[None, :] <= query_index[:, None]) & (row_ids[None, :] == my_ids[:, None])
+    allowed = (key_index[None, :] <= query_index[:, None]) & (
+        window_ids[None, :] == my_ids[:, None]
+    )
     scores = jnp.where(allowed[None, None], scores, NEGATIVE)
     fresh_max = jnp.maximum(running_max, jnp.max(scores, axis=-1))
     exps = jnp.exp(scores - fresh_max[..., None])
@@ -209,37 +218,46 @@
     )
     before = jnp.cumsum(route_hot, axis=0) - route_hot
     slot_index = jnp.sum(before * route_hot, axis=1)
-    buffer_index = flat_routes * capacity + slot_index
-    source = (
-        jnp.full((experts * capacity,), -1, jnp.int32)
-        .at[buffer_index]
-        .set(jnp.arange(tok_rows * TOP, dtype=jnp.int32))
-    )
-    filled = source >= 0
-    picked = jnp.take(moe_in, jnp.maximum(source, 0) // TOP, axis=0)
-    dispatch = jnp.where(filled[:, None], picked, jnp.zeros_like(picked)).reshape(
-        experts, capacity, model_width
+    slot_hot = (
+        slot_index[:, None] == jnp.arange(capacity, dtype=jnp.int32)[None, :]
+    ).astype(jnp.float32)
+    pair_hot = route_hot.astype(jnp.float32)[:, :, None] * slot_hot[:, None, :]
+    pair_hot = pair_hot.reshape(tok_rows, TOP, experts, capacity)
+    dispatch_hot = jnp.sum(pair_hot, axis=1).astype(jnp.bfloat16)
+    dispatch = jnp.einsum(
+        "tes,td->esd", dispatch_hot, moe_in, preferred_element_type=jnp.float32
+    ).astype(jnp.bfloat16)
+    combine = jnp.sum(
+        pair_hot * routing_gate_weight[:, :, None, None], axis=1
     )
     arrived = lax.all_to_all(dispatch, "expert", split_axis=0, concat_axis=0, tiled=True)
-    flat_rows = arrived.reshape(-1, model_width)
-    gate_out = multiply_rows(flat_rows, gate_up_full[0])
-    up_out = multiply_rows(flat_rows, gate_up_full[1])
+    gate_out = jnp.einsum(
+        "esd,fd->esf", arrived, gate_up_full[0], preferred_element_type=jnp.float32
+    )
+    up_out = jnp.einsum(
+        "esd,fd->esf", arrived, gate_up_full[1], preferred_element_type=jnp.float32
+    )
     activation = (jax.nn.silu(gate_out) * up_out).astype(jnp.bfloat16)
     block_units = expert_gate_up_weight.shape[1]
     block_count = down_full.shape[0] // block_units
-    summed = jnp.zeros((flat_rows.shape[0], model_width), jnp.float32)
+    summed = jnp.zeros(arrived.shape, jnp.float32)
     for quarter in range(block_count):
-        part = jnp.dot(
-            activation[:, quarter * block_units : (quarter + 1) * block_units],
+        part = jnp.einsum(
+            "esf,fd->esd",
+            activation[:, :, quarter * block_units : (quarter + 1) * block_units],
             down_full[quarter * block_units : (quarter + 1) * block_units],
             preferred_element_type=jnp.float32,
         )
         summed = summed + part.astype(jnp.bfloat16).astype(jnp.float32)
-    expert_rows = summed.astype(jnp.bfloat16).reshape(arrived.shape)
+    expert_rows = summed.astype(jnp.bfloat16)
     returned = lax.all_to_all(expert_rows, "expert", split_axis=0, concat_axis=0, tiled=True)
-    chosen = jnp.take(returned.reshape(experts * capacity, model_width), buffer_index, axis=0)
-    scaled = chosen.astype(jnp.float32) * routing_gate_weight.reshape(tok_rows * TOP)[:, None]
-    moe = jnp.sum(scaled.reshape(tok_rows, TOP, model_width), axis=1)
+    moe = jnp.einsum(
+        "tes,esd->td",
+        combine,
+        returned.astype(jnp.float32),
+        precision=lax.Precision.HIGHEST,
+        preferred_element_type=jnp.float32,
+    )
     return (mid.astype(jnp.float32) + moe).astype(jnp.bfloat16)
 
 

time: 570 us -> 523 us (0.918)
  blocking collectives: 84.5 us -> 147 us
  local copies, waits for them, and re-layouts: 109 us -> 53.1 us
  other arithmetic: 43.3 us -> 20.4 us
  waiting for transfers between devices: 204 us -> 191 us
  starting transfers between devices: 8.53 us -> 0.65 us
  matrix products: 96.5 us -> 90 us
    all_to_all x0 -> x1, blocking collectives: none -> 62.6 us  [shards(): lax.all_to_all(expert_rows, 'expert', split_axis=0, concat_axis=0, tiled=...]
    all_to_all x1 -> x0, waiting for transfers between devices: 55.3 us -> none  [shards(): lax.all_to_all(expert_rows, 'expert', split_axis=0, concat_axis=0, tiled=...]
    dot_general x4 -> x8, matrix products: 15.2 us -> 44 us  [the longest x4 16.5 us: shards(): jnp.einsum('esf,fd->esd', activation[:, :, quarter * block_units:(quarter...]
    gather x4 -> x0, local copies, waits for them, and re-layouts: 26.2 us -> none  [the longest x2 15.1 us: shards(): jnp.take(returned.reshape(experts * capacity, model_width), buffer_index,...]
    all_gather x1, waiting for transfers between devices: 40.7 us -> 66.5 us  [shards(): down_full = lax.all_gather(down_local, 'dp', axis=0, tiled=True)]
    reshape x4 -> x0, local copies, waits for them, and re-layouts: 19.6 us -> none  [the longest x1 6.53 us: shards(): flat_rows = arrived.reshape(-1, model_width)]
    dot_general x4 -> x2, matrix products: 22.3 us -> 4.22 us  [multiply_rows(): lax.dot_general(left, right, (((1,), (1,)), ((), ())), preferred_element_...]
    all_gather x1, waiting for transfers between devices: 0.01 us -> 17.1 us  [shards(): gate_up_full = lax.all_gather(gate_up_local, 'dp', axis=1, tiled=True)]
  transfers between devices with their start and end apart: 5 -> 4, of which waited for: 4 -> 4; matrix products, arithmetic and copies ran while one was open for 27% -> 21% of each run, Pallas kernels for 0% -> 0%
where the time goes in v2:
time: 523 us; the launch traced here: 516 us
  waiting for transfers between devices  191 us (37%)
  blocking collectives  147 us (28%)
  matrix products  90 us (17%)
  local copies, waits for them, and re-layouts  53.1 us (10%)
  other arithmetic  20.4 us (4%)
  between operations  14 us (3%)
    all_gather x1, waiting for transfers between devices, shards(): down_full = lax.all_gather(down_local, 'dp', axis=0, tiled=True)  66.5 us
    all_to_all x1, blocking collectives, shards(): lax.all_to_all(expert_rows, 'expert', split_axis=0, concat_axis=0, tiled=...  62.6 us
    all_gather x1, waiting for transfers between devices, shards(): all_factors = lax.all_gather(joined_factors, 'dp', axis=0, tiled=True)  59.6 us
    all_to_all x1, blocking collectives, shards(): lax.all_to_all(dispatch, 'expert', split_axis=0, concat_axis=0, tiled=True)  59.6 us
    all_gather x1, waiting for transfers between devices, shards(): lax.all_gather(jnp.concatenate([key_rows, value_rows], axis=1), 'expert',...  47.8 us
    all_gather x1, blocking collectives, shards(): row_ids = lax.all_gather(prompt_number, 'expert', axis=1, tiled=True)[0]  24.3 us
    unnamed x60, local copies, waits for them, and re-layouts  18.7 us
    dot_general x1, matrix products, shards(): jnp.einsum('tkgd,nkd->kgtn', queries, piece_keys, preferred_element_type=...  18.3 us
  transfers between devices with their start and end apart: 4, of which 4 were waited for; matrix products, arithmetic and copies ran while one was open for 21% of the time, Pallas kernels for 0%

profile of v2, /device:TPU:1, one launch (start us, length us, event | category | flops | bytes accessed | tf_op | source)
XLA Modules:
  0.0 515.9 jit_solution(9643417215440576231)
XLA Ops:
  6.5 2.6 reshape.396
  13.0 1.4 reshape.368
  17.2 24.3 %all_gather.15 = s32[1,4096]{1,0:T(1,128)S(1)} all-gather(s32[1,128]{1,0:T(1,128)S(1)} %copy-done.17), channel_id=1, replica_groups=mesh['dp'=4,'expert'=32] {'expert'}, dimensions={1}, use_global_device_ids=true | all-gather | bytes 16896 | tf_op jit(solution)/shard_map/all_gather | solution.py:87
  42.6 59.6 %all-gather.12.cloned.1.call-done = bf16[4,4,258048]{2,1,0:T(4,128)(2,1)} async-done(((bf16[1,4,258048]{2,1,0:T(4,128)(2,1)}), bf16[4,4,258048]{2,1,0:T(4,128)(2,1)}) %all-gather.12.cloned.1.call-update) | async-done | bytes 8257552 | tf_op jit(solution)/shard_map/all_gather | solution.py:105
  102.2 6.4 %reshape.378 = bf16[16,258048]{1,0:T(8,128)(2,1)} reshape(bf16[4,4,258048]{2,1,0:T(4,128)(2,1)} %all-gather.12.cloned.1.call-done) | data formatting | bytes 16515072
  108.6 3.8 slice.112
  112.4 6.7 %dot_general.57 = bf16[16,48,2880]{2,1,0:T(8,128)(2,1)} reshape(bf16[16,138240]{1,0:T(8,128)(2,1)} %slice.112) | data formatting | bytes 8847360 | tf_op jit(solution)/shard_map/dot_general | solution.py:38
  119.2 3.8 fusion.39
  124.5 47.8 %all-gather.6.cloned.1.call-done = bf16[4096,512]{1,0:T(8,128)(2,1)} async-done(((bf16[128,512]{1,0:T(8,128)(2,1)}), bf16[4096,512]{1,0:T(8,128)(2,1)}) %all-gather.6.cloned.1.call-update) | async-done | bytes 4194320 | tf_op jit(solution)/shard_map/all_gather | solution.py:156
  177.6 2.7 fusion.79
  180.9 1.4 convolution_add_fusion.1
  182.3 1.7 copy.64
  184.0 3.0 copy.87
  187.1 2.2 reshape_reshape.9
  190.2 4.3 fusion.80
  194.5 4.2 copy.63
  198.7 2.9 copy.65
  201.6 18.3 %fusion.81 = (f32[4,8,128]{2,1,0:T(8,128)S(1)}, f32[4,8,128,2176]{2,3,1,0:T(8,128)}) fusion(bf16[128,4,8,32]{0,3,2,1:T(8,128)(2,1)S(1)} %bitcast.140, bf16[128,4,8,32]{0,3,2,1:T(8,128)(2,1)S(1)} %bitcast.139, bf16[4096,4,64]{0,2,1:T(8,128)(2,1)} %bitcast.133, s32[]{:T(128)S(6)} %min.4, pred[128,2176]{0,1:T(8,128)(4,1)S(1)} %compare_and_fusion), kind=kOutput, calls=%fused_computation.138 | convolution fusion | flops 1168633856 | bytes 37584900 | tf_op jit(solution)/shard_map/tkgd,nkd->kgtn/dot_general | solution.py:177
  220.0 14.0 %fusion = f32[4,8,128]{2,1,0:T(8,128)S(1)} fusion(f32[4,8,128,2176]{2,3,1,0:T(8,128)} %get-tuple-element.29, f32[4,8,128]{2,1,0:T(8,128)S(1)} %broadcast_maximum_fusion), kind=kLoop, calls=%fused_computation.2 | loop fusion | flops 17821696 | bytes 35684352 | tf_op jit(solution)/shard_map/reduce_sum | solution.py:187
  234.1 14.5 %fusion.36 = bf16[128,4,8,64]{0,3,2,1:T(8,128)(2,1)S(1)} fusion(f32[4,8,128,2176]{2,3,1,0:T(8,128)} %get-tuple-element.29, f32[4,8,128]{2,1,0:T(8,128)S(1)} %broadcast_maximum_fusion, bf16[4096,4,64]{0,2,1:T(8,128)(2,1)S(1)} %bitcast.132, s32[]{:T(128)S(6)} %min.4, f32[128,4,8]{0,2,1:T(8,128)S(1)} %get-tuple-element.22, f32[128,4,8]{0,2,1:T(8,128)S(1)} %get-tuple-element.21), kind=kOutput, calls=%fused_computation.46 | convolution fusion | flops 1159462912 | bytes 37339140 | tf_op jit(solution)/shard_map/kgtn,nkd->kgtd/dot_general | solution.py:188
  249.1 6.4 %fusion.82 = f32[128,2880]{0,1:T(8,128)S(1)} fusion(bf16[2048,2880]{0,1:T(8,128)(2,1)} %param.32, bf16[128,2048]{0,1:T(8,128)(2,1)S(1)} %bitcast.147), kind=kOutput, calls=%fused_computation.139 | convolution fusion | flops 1509949440 | bytes 13795328 | tf_op jit(solution)/shard_map/dot_general | solution.py:204
  258.8 59.6 %all_to_all.10 = bf16[32,20,2880]{2,1,0:T(8,128)(2,1)} all-to-all(bf16[32,20,2880]{2,1,0:T(8,128)(2,1)S(1)} %copy.72), channel_id=1, replica_groups=mesh['dp'=4,'expert'=32] {'expert'}, dimensions={0} | all-to-all | bytes 7372800 | tf_op jit(solution)/shard_map/all_to_all | solution.py:233
  318.5 17.1 %all-gather.8.cloned.1.call-done = bf16[2,1536,2880]{1,2,0:T(8,128)(2,1)} async-done(((bf16[2,384,2880]{1,2,0:T(8,128)(2,1)}), bf16[2,1536,2880]{1,2,0:T(8,128)(2,1)}) %all-gather.8.cloned.1.call-update) | async-done | bytes 17694736 | tf_op jit(solution)/shard_map/all_gather | solution.py:166
  335.5 12.7 %fusion.6 = f32[32,20,1536]{2,0,1:T(8,128)} fusion(bf16[2,1536,2880]{1,2,0:T(8,128)(2,1)} %all-gather.8.cloned.1.call-done, bf16[32,20,2880]{2,1,0:T(8,128)(2,1)} %all_to_all.10), kind=kOutput, calls=%fused_computation.9 | convolution fusion | flops 5662310400 | bytes 17301504 | tf_op jit(solution)/shard_map/esd,fd->esf/dot_general | solution.py:234
  348.7 8.6 %multiply_convert_fusion = bf16[32,20,1536]{2,0,1:T(8,128)(2,1)S(1)} fusion(f32[32,20,1536]{2,0,1:T(8,128)} %fusion.6, bf16[2,1536,2880]{1,2,0:T(8,128)(2,1)S(1)} %copy-done.21, bf16[32,20,2880]{2,1,0:T(8,128)(2,1)S(1)} %copy-done.3), kind=kOutput, calls=%fused_computation.16 | convolution fusion | flops 5668208640 | bytes 19267584 | tf_op jit(solution)/shard_map/esd,fd->esf/dot_general | solution.py:237
  357.3 66.5 %all-gather.10.cloned.1.call-done = bf16[1536,2880]{0,1:T(8,128)(2,1)} async-done(((bf16[384,2880]{0,1:T(8,128)(2,1)}), bf16[1536,2880]{0,1:T(8,128)(2,1)}) %all-gather.10.cloned.1.call-update) | async-done | bytes 8847376 | tf_op jit(solution)/shard_map/all_gather | solution.py:167
  423.9 4.0 convolution_convert_fusion.2
  427.8 3.8 convolution_convert_fusion.1
  431.7 4.0 convolution_convert_fusion
  435.7 4.7 add_convert_fusion
  441.5 62.6 %all_to_all.11 = bf16[32,20,2880]{2,1,0:T(8,128)(2,1)S(1)} all-to-all(bf16[32,20,2880]{2,1,0:T(8,128)(2,1)S(1)} %copy.75), channel_id=1, replica_groups=mesh['dp'=4,'expert'=32] {'expert'}, dimensions={0} | all-to-all | bytes 7372800 | tf_op jit(solution)/shard_map/all_to_all | solution.py:253
  504.1 4.9 fusion.18
  (122 shorter events, 21.3 us)
Async XLA Ops:
  6.5 3.5 copy-start.12
  6.5 95.7 %all-gather.12.cloned.1.call-start = ((), (), s32[]{:S(2)}) async-start(), calls=%async_computation.5 | async-start | bytes 10321920 | tf_op jit(solution)/shard_map/all_gather | solution.py:105
  9.5 7.6 %copy-start.17 = (s32[1,128]{1,0:T(1,128)S(1)}, s32[1,128]{1,0:T(1,128)}, u32[]{:S(2)}) copy-start(s32[1,128]{1,0:T(1,128)} %param.23) | copy-start | bytes 1540
  9.5 32.4 %copy-start.19 = (s32[1,16]{1,0:T(1,128)S(1)}, s32[1,16]{1,0:T(1,128)}, u32[]{:S(2)}) copy-start(s32[1,16]{1,0:T(1,128)} %param.24) | copy-start | bytes 196
  10.0 32.0 %copy-start.4 = (bf16[128,2880]{0,1:T(8,128)(2,1)S(1)}, bf16[128,2880]{0,1:T(8,128)(2,1)}, u32[]{:S(2)}) copy-start(bf16[128,2880]{0,1:T(8,128)(2,1)} %param.19) | copy-start | bytes 2211844
  15.7 1.3 copy-start.2
  17.1 155.2 %all-gather.6.cloned.1.call-start = ((), (), s32[]{:S(2)}) async-start(), calls=%async_computation.2 | async-start | bytes 4325376 | tf_op jit(solution)/shard_map/all_gather | solution.py:156
  112.4 6.7 %copy-start.23 = (f32[2880]{0:T(1024)S(1)}, f32[2880]{0:T(1024)}, u32[]{:S(2)}) copy-start(f32[2880]{0:T(1024)} %param.26) | copy-start | bytes 34564
  119.1 3.8 slice-start
  119.1 3.9 copy-start.14
  119.2 4.4 copy-start.13
  122.9 50.0 %copy-start.16 = (s32[128,4]{0,1:T(4,128)S(1)}, s32[128,4]{0,1:T(4,128)}, u32[]{:S(2)}) copy-start(s32[128,4]{0,1:T(4,128)} %param.36) | copy-start | bytes 6148
  123.0 50.3 %copy-start.20 = (f32[32]{0:T(128)S(1)}, f32[32]{0:T(128)}, u32[]{:S(2)}) copy-start(f32[32]{0:T(128)} %param.25) | copy-start | bytes 388
  123.0 52.3 %copy-start.18 = (f32[128,4]{0,1:T(4,128)S(1)}, f32[128,4]{0,1:T(4,128)}, u32[]{:S(2)}) copy-start(f32[128,4]{0,1:T(4,128)} %param.37) | copy-start | bytes 6148
  124.5 211.0 %all-gather.8.cloned.1.call-start = ((), (), s32[]{:S(2)}) async-start(), calls=%async_computation.3 | async-start | bytes 22118400 | tf_op jit(solution)/shard_map/all_gather | solution.py:166
  172.4 251.5 %all-gather.10.cloned.1.call-start = ((), (), s32[]{:S(2)}) async-start(), calls=%async_computation.4 | async-start | bytes 11059200 | tf_op jit(solution)/shard_map/all_gather | solution.py:167
  177.6 3.3 copy-start.11
  180.9 6.2 %slice-start.1 = ((bf16[16,258048]{1,0:T(8,128)(2,1)}), bf16[16,46080]{1,0:T(8,128)(2,1)S(1)}, s32[]{:S(2)}) async-start(bf16[16,258048]{1,0:T(8,128)(2,1)} %reshape.378), calls=%async_computation.7 | async-start | bytes 2949120 | tf_op jit(solution)/shard_map/slice | solution.py:111
  194.5 7.1 %copy-start.7 = (bf16[128,32,32]{0,2,1:T(8,128)(2,1)S(1)}, bf16[128,32,32]{0,2,1:T(8,128)(2,1)}, u32[]{:S(2)}) copy-start(bf16[128,32,32]{0,2,1:T(8,128)(2,1)} %get-tuple-element.17) | copy-start | bytes 786436
  194.5 7.1 %copy-start.8 = (bf16[128,32,32]{0,2,1:T(8,128)(2,1)S(1)}, bf16[128,32,32]{0,2,1:T(8,128)(2,1)}, u32[]{:S(2)}) copy-start(bf16[128,32,32]{0,2,1:T(8,128)(2,1)} %get-tuple-element.18) | copy-start | bytes 786436
  220.0 14.1 %copy-start.1 = (bf16[4096,256]{0,1:T(8,128)(2,1)S(1)}, bf16[4096,256]{0,1:T(8,128)(2,1)}, u32[]{:S(2)}) copy-start(bf16[4096,256]{0,1:T(8,128)(2,1)} %copy.65) | copy-start | bytes 6291460
  234.1 14.5 %copy-start.9 = (bf16[2,8,16,2048]{3,2,1,0:T(8,128)(2,1)S(1)}, bf16[2,8,16,2048]{3,2,1,0:T(8,128)(2,1)}, u32[]{:S(2)}) copy-start(bf16[2,8,16,2048]{3,2,1,0:T(8,128)(2,1)} %copy.87) | copy-start | bytes 3145732
  249.1 6.5 %copy-start = (bf16[256,2880]{1,0:T(8,128)(2,1)S(1)}, bf16[256,2880]{1,0:T(8,128)(2,1)}, u32[]{:S(2)}) copy-start(bf16[256,2880]{1,0:T(8,128)(2,1)} %reshape_reshape.9) | copy-start | bytes 4423684
  249.1 6.5 %copy-start.5 = (bf16[128,2880]{0,1:T(8,128)(2,1)S(1)}, bf16[128,2880]{0,1:T(8,128)(2,1)}, u32[]{:S(2)}) copy-start(bf16[128,2880]{0,1:T(8,128)(2,1)} %param.19) | copy-start | bytes 2211844
  255.5 0.9 copy-start.10
  255.5 0.9 copy-start.15
  335.5 12.7 %copy-start.3 = (bf16[32,20,2880]{2,1,0:T(8,128)(2,1)S(1)}, bf16[32,20,2880]{2,1,0:T(8,128)(2,1)}, u32[]{:S(2)}) copy-start(bf16[32,20,2880]{2,1,0:T(8,128)(2,1)} %all_to_all.10) | copy-start | bytes 11059204
  335.5 13.2 %copy-start.21 = (bf16[2,1536,2880]{1,2,0:T(8,128)(2,1)S(1)}, bf16[2,1536,2880]{1,2,0:T(8,128)(2,1)}, u32[]{:S(2)}) copy-start(bf16[2,1536,2880]{1,2,0:T(8,128)(2,1)} %all-gather.8.cloned.1.call-done) | copy-start | bytes 53084164
  423.9 7.8 %copy-start.22 = (bf16[1536,2880]{0,1:T(8,128)(2,1)S(1)}, bf16[1536,2880]{0,1:T(8,128)(2,1)}, u32[]{:S(2)}) copy-start(bf16[1536,2880]{0,1:T(8,128)(2,1)} %all-gather.10.cloned.1.call-done) | copy-start | bytes 26542084
  441.5 62.6 %copy-start.6 = (f32[128,32,20]{0,1,2:T(8,128)S(1)}, f32[128,32,20]{0,1,2:T(8,128)}, u32[]{:S(2)}) copy-start(f32[128,32,20]{0,1,2:T(8,128)} %get-tuple-element.10) | copy-start | bytes 983044
Sparse Core Ops, SparseCore 0:
  17.2 84.9 all-gather.11
  124.6 47.6 all-gather.5
  174.0 161.4 all-gather.7
  337.1 86.7 all-gather.9

commit v3 on v2

--- a/solution.py
+++ b/solution.py
@@ -54,6 +54,31 @@
     gate_out = multiply_rows(rows_in, gate_up[:, 0, :])
     up_out = multiply_rows(rows_in, gate_up[:, 1, :])
     return (jax.nn.silu(gate_out) * up_out).astype(jnp.bfloat16)
+
+
+def gather_expert_blocks(gate_up_local, down_local, anchor=None):
+    count = lax.axis_size("dp")
+    if count != 4:
+        gate_up_full = lax.all_gather(gate_up_local, "dp", axis=1, tiled=True)
+        down_full = lax.all_gather(down_local, "dp", axis=0, tiled=True)
+        return anchor, [(gate_up_full[0], gate_up_full[1], [down_full])]
+    forward = [(i, (i + 1) % count) for i in range(count)]
+    backward = [(i, (i - 1) % count) for i in range(count)]
+    gate_up_prev, down_prev = lax.ppermute((gate_up_local, down_local), "dp", forward)
+    gate_up_next, down_next = lax.ppermute((gate_up_local, down_local), "dp", backward)
+    if anchor is not None:
+        anchor, gate_up_prev, down_prev, gate_up_next, down_next = lax.optimization_barrier(
+            (anchor, gate_up_prev, down_prev, gate_up_next, down_next)
+        )
+    half = down_local.shape[0] // 2
+    far_gate, far_down_a = lax.ppermute((gate_up_prev[0], down_prev[:half]), "dp", forward)
+    far_up, far_down_b = lax.ppermute((gate_up_next[1], down_next[half:]), "dp", backward)
+    return anchor, [
+        (gate_up_local[0], gate_up_local[1], [down_local]),
+        (gate_up_prev[0], gate_up_prev[1], [down_prev]),
+        (gate_up_next[0], gate_up_next[1], [down_next]),
+        (far_gate, far_up, [far_down_a, far_down_b]),
+    ]
 
 
 def shards(
@@ -112,6 +137,10 @@
         )
         offset += width
     all_down, all_up_query, all_up_keyval, all_o_down, all_o_up = factors
+    gate_up_local = jnp.transpose(expert_gate_up_weight[0], (1, 0, 2))
+    gate_up_local, down_local, _ = lax.optimization_barrier(
+        (gate_up_local, expert_down_weight[0], all_factors)
+    )
     adapter_table = all_down.shape[0]
     adapter_selector = (
         adapter_of[:, None] == jnp.arange(adapter_table, dtype=jnp.int32)[None, :]
@@ -160,11 +189,6 @@
     piece_keys = piece_kv[:, :kv_width].reshape(piece_rows, kv_heads, HD)
     piece_values = piece_kv[:, kv_width:].reshape(piece_rows, kv_heads, HD)
     gate_up_local = jnp.transpose(expert_gate_up_weight[0], (1, 0, 2))
-    gate_up_local, down_local, _ = lax.optimization_barrier(
-        (gate_up_local, expert_down_weight[0], piece_kv)
-    )
-    gate_up_full = lax.all_gather(gate_up_local, "dp", axis=1, tiled=True)
-    down_full = lax.all_gather(down_local, "dp", axis=0, tiled=True)
     window = min(piece_rows, piece_rows // 2 + tok_rows)
     window_start = jnp.clip(
         (lax.axis_index("expert") + 1) * tok_rows - window, 0, piece_rows - window
@@ -196,6 +220,7 @@
         .reshape(tok_rows, q_width)
         .astype(jnp.bfloat16)
     )
+    attended, expert_blocks = gather_expert_blocks(gate_up_local, down_local, attended)
     o_low = select_adapter(
         multiply_rows(attended, all_o_down.reshape(adapter_table * ADAPTER_RANK, q_width)),
         adapter_selector,
@@ -231,23 +256,21 @@
         pair_hot * routing_gate_weight[:, :, None, None], axis=1
     )
     arrived = lax.all_to_all(dispatch, "expert", split_axis=0, concat_axis=0, tiled=True)
-    gate_out = jnp.einsum(
-        "esd,fd->esf", arrived, gate_up_full[0], preferred_element_type=jnp.float32
-    )
-    up_out = jnp.einsum(
-        "esd,fd->esf", arrived, gate_up_full[1], preferred_element_type=jnp.float32
-    )
-    activation = (jax.nn.silu(gate_out) * up_out).astype(jnp.bfloat16)
-    block_units = expert_gate_up_weight.shape[1]
-    block_count = down_full.shape[0] // block_units
     summed = jnp.zeros(arrived.shape, jnp.float32)
-    for quarter in range(block_count):
-        part = jnp.einsum(
-            "esf,fd->esd",
-            activation[:, :, quarter * block_units : (quarter + 1) * block_units],
-            down_full[quarter * block_units : (quarter + 1) * block_units],
-            preferred_element_type=jnp.float32,
-        )
+    for gate_w, up_w, down_ws in expert_blocks:
+        gate_out = jnp.einsum("esd,fd->esf", arrived, gate_w, preferred_element_type=jnp.float32)
+        up_out = jnp.einsum("esd,fd->esf", arrived, up_w, preferred_element_type=jnp.float32)
+        activation = (jax.nn.silu(gate_out) * up_out).astype(jnp.bfloat16)
+        part = jnp.zeros(arrived.shape, jnp.float32)
+        offset = 0
+        for down_w in down_ws:
+            part = part + jnp.einsum(
+                "esf,fd->esd",
+                activation[:, :, offset : offset + down_w.shape[0]],
+                down_w,
+                preferred_element_type=jnp.float32,
+            )
+            offset += down_w.shape[0]
         summed = summed + part.astype(jnp.bfloat16).astype(jnp.float32)
     expert_rows = summed.astype(jnp.bfloat16)
     returned = lax.all_to_all(expert_rows, "expert", split_axis=0, concat_axis=0, tiled=True)

time: 523 us -> 513 us (0.981)
  blocking collectives: 147 us -> 85.9 us
  matrix products: 90 us -> 114 us
  starting transfers between devices: 0.65 us -> 16.8 us
  local copies, waits for them, and re-layouts: 53.1 us -> 63.6 us
    all_gather x2 -> x0, waiting for transfers between devices: 83.6 us -> none  [the longest x1 66.5 us: shards(): down_full = lax.all_gather(down_local, 'dp', axis=0, tiled=True)]
    all_to_all x1 -> x0, blocking collectives: 59.6 us -> none  [shards(): lax.all_to_all(dispatch, 'expert', split_axis=0, concat_axis=0, tiled=True)]
    all_gather x1, waiting for transfers between devices: 59.6 us -> 119 us  [shards(): all_factors = lax.all_gather(joined_factors, 'dp', axis=0, tiled=True)]
    all_to_all x0 -> x1, waiting for transfers between devices: none -> 37.5 us  [shards(): lax.all_to_all(dispatch, 'expert', split_axis=0, concat_axis=0, tiled=True)]
    dot_general x6 -> x13, matrix products: 37.8 us -> 61.5 us  [the longest x4 22.4 us: shards(): jnp.einsum('esd,fd->esf', arrived, up_w, preferred_element_type=jnp.float32)]
    all_gather x1, waiting for transfers between devices: 47.8 us -> 32.9 us  [shards(): lax.all_gather(jnp.concatenate([key_rows, value_rows], axis=1), 'expert',...]
    ppermute x0 -> x8, starting transfers between devices: none -> 11.4 us  [the longest x2 5.09 us: gather_expert_blocks(): lax.ppermute((gate_up_next[1], down_next[half:]), 'dp', backward)]
    slice x1 -> x6, local copies, waits for them, and re-layouts: 0.22 us -> 7.35 us  [the longest x2 3.75 us: gather_expert_blocks(): down_next[half:]]
  transfers between devices with their start and end apart: 4 -> 11, of which waited for: 4 -> 3; matrix products, arithmetic and copies ran while one was open for 21% -> 33% of each run, Pallas kernels for 0% -> 0%
where the time goes in v3:
time: 513 us; the launch traced here: 504 us
  waiting for transfers between devices  189 us (37%)
  matrix products  114 us (22%)
  blocking collectives  85.9 us (17%)
  local copies, waits for them, and re-layouts  63.6 us (12%)
  other arithmetic  20.1 us (4%)
  starting transfers between devices  16.8 us (3%)
  between operations  14.3 us (3%)
    all_gather x1, waiting for transfers between devices, shards(): all_factors = lax.all_gather(joined_factors, 'dp', axis=0, tiled=True)  119 us
    all_to_all x1, blocking collectives, shards(): lax.all_to_all(expert_rows, 'expert', split_axis=0, concat_axis=0, tiled=...  61.7 us
    all_to_all x1, waiting for transfers between devices, shards(): lax.all_to_all(dispatch, 'expert', split_axis=0, concat_axis=0, tiled=True)  37.5 us
    all_gather x1, waiting for transfers between devices, shards(): lax.all_gather(jnp.concatenate([key_rows, value_rows], axis=1), 'expert',...  32.9 us
    all_gather x1, blocking collectives, shards(): row_ids = lax.all_gather(prompt_number, 'expert', axis=1, tiled=True)[0]  24.2 us
    dot_general x4, matrix products, shards(): jnp.einsum('esd,fd->esf', arrived, up_w, preferred_element_type=jnp.float32)  22.4 us
    dot_general x4, matrix products, shards(): jnp.einsum('esd,fd->esf', arrived, gate_w, preferred_element_type=jnp.flo...  20.6 us
    dot_general x5, matrix products, shards(): jnp.einsum('esf,fd->esd', activation[:, :, offset:offset + down_w.shape[0...  18.5 us
  transfers between devices with their start and end apart: 11, of which 3 were waited for; matrix products, arithmetic and copies ran while one was open for 33% of the time, Pallas kernels for 0%

profile of v3, /device:TPU:1, one launch (start us, length us, event | category | flops | bytes accessed | tf_op | source)
XLA Modules:
  0.0 504.0 jit_solution(7609402195340386535)
XLA Ops:
  17.8 24.2 %all_gather.9 = s32[1,4096]{1,0:T(1,128)S(1)} all-gather(s32[1,128]{1,0:T(1,128)S(1)} %copy-done.16), channel_id=1, replica_groups=mesh['dp'=4,'expert'=32] {'expert'}, dimensions={1}, use_global_device_ids=true | all-gather | bytes 16896 | tf_op jit(solution)/shard_map/all_gather | solution.py:112
  47.1 118.6 %all-gather.6.cloned.1.call-done = bf16[4,4,258048]{2,1,0:T(4,128)(2,1)} async-done(((bf16[1,4,258048]{2,1,0:T(4,128)(2,1)}), bf16[4,4,258048]{2,1,0:T(4,128)(2,1)}) %all-gather.6.cloned.1.call-update) | async-done | bytes 8257552 | tf_op jit(solution)/shard_map/all_gather | solution.py:130
  165.7 6.4 %reshape.377 = bf16[16,258048]{1,0:T(8,128)(2,1)} reshape(bf16[4,4,258048]{2,1,0:T(4,128)(2,1)} %all-gather.6.cloned.1.call-done) | data formatting | bytes 16515072
  172.1 3.8 slice.114
  175.9 6.7 %dot_general.78 = bf16[16,48,2880]{2,1,0:T(8,128)(2,1)} reshape(bf16[16,138240]{1,0:T(8,128)(2,1)} %slice.114) | data formatting | bytes 8847360 | tf_op jit(solution)/shard_map/dot_general | solution.py:38
  182.7 3.8 fusion.58
  202.8 32.9 %all-gather.4.cloned.1.call-done = bf16[4096,512]{1,0:T(8,128)(2,1)} async-done(((bf16[128,512]{1,0:T(8,128)(2,1)}), bf16[4096,512]{1,0:T(8,128)(2,1)}) %all-gather.4.cloned.1.call-update) | async-done | bytes 4194320 | tf_op jit(solution)/shard_map/all_gather | solution.py:185
  235.6 3.8 fusion.104
  239.5 4.1 copy.96
  243.6 18.1 %fusion.106 = (f32[4,8,128]{2,1,0:T(8,128)S(1)}, f32[4,8,128,2176]{2,3,1,0:T(8,128)}) fusion(bf16[128,4,8,32]{0,3,2,1:T(8,128)(2,1)S(1)} %bitcast.183, bf16[128,4,8,32]{0,3,2,1:T(8,128)(2,1)S(1)} %bitcast.182, bf16[4096,4,64]{0,2,1:T(8,128)(2,1)} %bitcast.176, s32[]{:T(128)S(6)} %min.4, pred[128,2176]{0,1:T(8,128)(4,1)S(1)} %compare_and_fusion), kind=kOutput, calls=%fused_computation.163 | convolution fusion | flops 1168633856 | bytes 37584900 | tf_op jit(solution)/shard_map/tkgd,nkd->kgtn/dot_general | solution.py:201
  261.8 13.6 %fusion = f32[4,8,128]{2,1,0:T(8,128)S(1)} fusion(f32[4,8,128,2176]{2,3,1,0:T(8,128)} %get-tuple-element.39, f32[4,8,128]{2,1,0:T(8,128)S(1)} %broadcast_maximum_fusion), kind=kLoop, calls=%fused_computation.2 | loop fusion | flops 17821696 | bytes 35684352 | tf_op jit(solution)/shard_map/reduce_sum | solution.py:211
  278.4 14.4 %fusion.55 = bf16[128,4,8,64]{0,3,2,1:T(8,128)(2,1)S(1)} fusion(f32[4,8,128,2176]{2,3,1,0:T(8,128)} %get-tuple-element.39, f32[4,8,128]{2,1,0:T(8,128)S(1)} %broadcast_maximum_fusion, bf16[4096,4,64]{0,2,1:T(8,128)(2,1)} %bitcast.175, s32[]{:T(128)S(6)} %min.4, f32[128,4,8]{0,2,1:T(8,128)S(1)} %get-tuple-element.32, f32[128,4,8]{0,2,1:T(8,128)S(1)} %get-tuple-element.31), kind=kOutput, calls=%fused_computation.62 | convolution fusion | flops 1159462912 | bytes 37339140 | tf_op jit(solution)/shard_map/kgtn,nkd->kgtd/dot_general | solution.py:212
  294.9 6.4 %multiply_reduce_fusion.1 = (f32[128]{0:T(128)S(1)}, f32[128,2880]{0,1:T(8,128)S(1)}) fusion(f32[128,2880]{0,1:T(8,128)S(1)} %fusion.107, bf16[2048,2880]{0,1:T(8,128)(2,1)} %param.32, bf16[128,2048]{0,1:T(8,128)(2,1)S(1)} %bitcast.181, bf16[128,2880]{0,1:T(8,128)(2,1)S(1)} %copy-done.3), kind=kOutput, calls=%fused_computation.55 | convolution fusion | flops 1512529792 | bytes 16007680 | tf_op jit(solution)/shard_map/dot_general | solution.py:229
  302.6 3.3 copy.105
  305.9 5.4 %all-to-all-start = ((bf16[32,20,2880]{2,1,0:T(8,128)(2,1)}), bf16[32,20,2880]{2,1,0:T(8,128)(2,1)}, u32[]{:S(2)}, u32[]{:S(2)}) async-start(bf16[32,20,2880]{2,1,0:T(8,128)(2,1)} %copy.105), calls=%async_computation | async-start | bytes 9043968 | tf_op jit(solution)/shard_map/all_to_all | solution.py:258
  317.4 3.2 slice_bitcast_fusion.5
  320.6 3.3 slice_bitcast_fusion.4
  329.8 37.5 %all-to-all-done = bf16[32,20,2880]{2,1,0:T(8,128)(2,1)} async-done(((bf16[32,20,2880]{2,1,0:T(8,128)(2,1)}), bf16[32,20,2880]{2,1,0:T(8,128)(2,1)}, u32[]{:S(2)}, u32[]{:S(2)}) %all-to-all-start) | async-done | bytes 3686432 | tf_op jit(solution)/shard_map/all_to_all | solution.py:258
  367.3 5.3 %fusion.28 = f32[32,20,384]{2,1,0:T(8,128)S(1)} fusion(bf16[32,20,2880]{2,1,0:T(8,128)(2,1)} %all-to-all-done, bf16[2,384,2880]{1,2,0:T(8,128)(2,1)} %collective-permute-done.2), kind=kOutput, calls=%fused_computation.33 | convolution fusion | flops 1415577600 | bytes 7716864 | tf_op jit(solution)/shard_map/esd,fd->esf/dot_general | solution.py:261
  372.6 5.2 %fusion.33 = f32[32,20,384]{2,1,0:T(8,128)S(1)} fusion(bf16[32,20,2880]{2,1,0:T(8,128)(2,1)} %all-to-all-done, bf16[2,384,2880]{1,2,0:T(8,128)(2,1)} %collective-permute-done), kind=kOutput, calls=%fused_computation.38 | convolution fusion | flops 1415577600 | bytes 7716864 | tf_op jit(solution)/shard_map/esd,fd->esf/dot_general | solution.py:261
  377.8 4.5 fusion.20
  382.4 5.6 %fusion.23 = f32[32,20,384]{2,1,0:T(8,128)S(1)} fusion(bf16[32,20,2880]{2,1,0:T(8,128)(2,1)} %all-to-all-done, bf16[384,2880]{0,1:T(8,128)(2,1)} %collective-permute-done.4), kind=kOutput, calls=%fused_computation.28 | convolution fusion | flops 1415577600 | bytes 6881280 | tf_op jit(solution)/shard_map/esd,fd->esf/dot_general | solution.py:261
  387.9 5.8 %multiply_convert_fusion.2 = bf16[32,20,384]{2,1,0:T(8,128)(2,1)S(1)} fusion(f32[32,20,384]{2,1,0:T(8,128)S(1)} %fusion.28, bf16[32,20,2880]{2,1,0:T(8,128)(2,1)} %all-to-all-done, bf16[2,384,2880]{1,2,0:T(8,128)(2,1)} %collective-permute-done.2), kind=kOutput, calls=%fused_computation.65 | convolution fusion | flops 1417052160 | bytes 8208384 | tf_op jit(solution)/shard_map/esd,fd->esf/dot_general | solution.py:262
  393.7 5.8 %multiply_convert_fusion.3 = bf16[32,20,384]{2,1,0:T(8,128)(2,1)S(1)} fusion(f32[32,20,384]{2,1,0:T(8,128)S(1)} %fusion.33, bf16[32,20,2880]{2,1,0:T(8,128)(2,1)} %all-to-all-done, bf16[2,384,2880]{1,2,0:T(8,128)(2,1)} %collective-permute-done), kind=kOutput, calls=%fused_computation.66 | convolution fusion | flops 1417052160 | bytes 8208384 | tf_op jit(solution)/shard_map/esd,fd->esf/dot_general | solution.py:262
  399.5 5.1 %fusion.50 = bf16[32,20,384]{2,1,0:T(8,128)(2,1)S(1)} fusion(bf16[32,20,2880]{2,1,0:T(8,128)(2,1)} %all-to-all-done, bf16[2,384,2880]{1,2,0:T(8,128)(2,1)S(1)} %bitcast.207, f32[32,20,384]{2,1,0:T(8,128)S(1)} %fusion.20), kind=kOutput, calls=%fused_computation.59 | convolution fusion | flops 1417052160 | bytes 7569408 | tf_op jit(solution)/shard_map/esd,fd->esf/dot_general | solution.py:262
  404.6 5.8 %multiply_convert_fusion.1 = bf16[32,20,384]{2,1,0:T(8,128)(2,1)S(1)} fusion(f32[32,20,384]{2,1,0:T(8,128)S(1)} %fusion.23, bf16[32,20,2880]{2,1,0:T(8,128)(2,1)} %all-to-all-done, bf16[384,2880]{0,1:T(8,128)(2,1)} %collective-permute-done.5), kind=kOutput, calls=%fused_computation.64 | convolution fusion | flops 1417052160 | bytes 7372800 | tf_op jit(solution)/shard_map/esd,fd->esf/dot_general | solution.py:262
  410.3 3.8 convolution_convert_fusion
  414.2 4.0 convolution_convert_fusion.1
  418.4 4.2 convolution_convert_fusion.2
  425.0 4.1 add_convert_fusion
  430.3 61.7 %all_to_all.10 = bf16[32,20,2880]{2,1,0:T(8,128)(2,1)S(1)} all-to-all(bf16[32,20,2880]{2,1,0:T(8,128)(2,1)S(1)} %copy.113), channel_id=1, replica_groups=mesh['dp'=4,'expert'=32] {'expert'}, dimensions={0} | all-to-all | bytes 7372800 | tf_op jit(solution)/shard_map/all_to_all | solution.py:276
  492.0 4.9 fusion.13
  (146 shorter events, 54.5 us)
Async XLA Ops:
  6.5 159.2 %all-gather.6.cloned.1.call-start = ((), (), s32[]{:S(2)}) async-start(), calls=%async_computation.3 | async-start | bytes 10321920 | tf_op jit(solution)/shard_map/all_gather | solution.py:130
  10.7 6.7 %copy-start.15 = (s32[128,4]{0,1:T(4,128)S(1)}, s32[128,4]{0,1:T(4,128)}, u32[]{:S(2)}) copy-start(s32[128,4]{0,1:T(4,128)} %param.36) | copy-start | bytes 6148
  12.1 5.7 %copy-start.16 = (s32[1,128]{1,0:T(1,128)S(1)}, s32[1,128]{1,0:T(1,128)}, u32[]{:S(2)}) copy-start(s32[1,128]{1,0:T(1,128)} %param.23) | copy-start | bytes 1540
  12.2 32.8 %copy-start.18 = (s32[1,16]{1,0:T(1,128)S(1)}, s32[1,16]{1,0:T(1,128)}, u32[]{:S(2)}) copy-start(s32[1,16]{1,0:T(1,128)} %param.24) | copy-start | bytes 196
  12.2 32.9 %copy-start.2 = (bf16[128,2880]{0,1:T(8,128)(2,1)S(1)}, bf16[128,2880]{0,1:T(8,128)(2,1)}, u32[]{:S(2)}) copy-start(bf16[128,2880]{0,1:T(8,128)(2,1)} %param.19) | copy-start | bytes 2211844
  13.9 221.7 %all-gather.4.cloned.1.call-start = ((), (), s32[]{:S(2)}) async-start(), calls=%async_computation.2 | async-start | bytes 4325376 | tf_op jit(solution)/shard_map/all_gather | solution.py:185
  14.0 278.8 %collective-permute-start = (bf16[2,384,2880]{1,2,0:T(8,128)(2,1)}, bf16[2,384,2880]{1,2,0:T(8,128)(2,1)}, u32[]{:S(2)}, u32[]{:S(2)}) collective-permute-start(bf16[2,384,2880]{1,2,0:T(8,128)(2,1)} %bitcast.202), channel_id=1, source_target_pairs={{0,32},{32,64},{64,96},{96,0},{1,33},{33,65},{65,97},{97,1},{2,34}... | collective-permute-start | bytes 13271048 | tf_op jit(solution)/shard_map/ppermute | solution.py:67
  16.1 276.7 %collective-permute-start.2 = (bf16[2,384,2880]{1,2,0:T(8,128)(2,1)}, bf16[2,384,2880]{1,2,0:T(8,128)(2,1)}, u32[]{:S(2)}, u32[]{:S(2)}) collective-permute-start(bf16[2,384,2880]{1,2,0:T(8,128)(2,1)} %bitcast.203), channel_id=1, source_target_pairs={{0,96},{32,0},{64,32},{96,64},{1,97},{33,1},{65,33},{97,65},{2,98}... | collective-permute-start | bytes 13271048 | tf_op jit(solution)/shard_map/ppermute | solution.py:68
  175.9 6.7 %copy-start.20 = (f32[2880]{0:T(1024)S(1)}, f32[2880]{0:T(1024)}, u32[]{:S(2)}) copy-start(f32[2880]{0:T(1024)} %param.26) | copy-start | bytes 34564
  182.7 3.8 slice-start
  182.7 3.9 copy-start.13
  182.7 4.4 copy-start.11
  186.5 1.5 copy-start.17
  188.9 103.9 %collective-permute-start.1 = (bf16[384,2880]{0,1:T(8,128)(2,1)}, bf16[384,2880]{0,1:T(8,128)(2,1)}, u32[]{:S(2)}, u32[]{:S(2)}) collective-permute-start(bf16[384,2880]{0,1:T(8,128)(2,1)} %bitcast.208), channel_id=1, source_target_pairs={{0,32},{32,64},{64,96},{96,0},{1,33},{33,65},{65,97},{97,1},{2,34}... | collective-permute-start | bytes 6635528 | tf_op jit(solution)/shard_map/ppermute | solution.py:67
  190.1 102.7 %collective-permute-start.3 = (bf16[384,2880]{0,1:T(8,128)(2,1)}, bf16[384,2880]{0,1:T(8,128)(2,1)}, u32[]{:S(2)}, u32[]{:S(2)}) collective-permute-start(bf16[384,2880]{0,1:T(8,128)(2,1)} %bitcast.209), channel_id=1, source_target_pairs={{0,96},{32,0},{64,32},{96,64},{1,97},{33,1},{65,33},{97,65},{2,98}... | collective-permute-start | bytes 6635528 | tf_op jit(solution)/shard_map/ppermute | solution.py:68
  195.5 4.1 slice-start.1
  239.5 4.1 copy-start.5
  239.5 4.1 copy-start.6
  278.4 14.4 %copy-start.7 = (bf16[2,8,16,2048]{3,2,1,0:T(8,128)(2,1)S(1)}, bf16[2,8,16,2048]{3,2,1,0:T(8,128)(2,1)}, u32[]{:S(2)}) copy-start(bf16[2,8,16,2048]{3,2,1,0:T(8,128)(2,1)} %copy.125) | copy-start | bytes 3145732
  292.8 1.4 copy-start
  293.3 1.7 copy-start.3
  294.9 6.4 %copy-start.8 = (bf16[128,32,20]{0,1,2:T(8,128)(2,1)S(1)}, bf16[128,32,20]{0,1,2:T(8,128)(2,1)}, u32[]{:S(2)}) copy-start(bf16[128,32,20]{0,1,2:T(8,128)(2,1)} %get-tuple-element.17) | copy-start | bytes 491524
  294.9 6.4 %copy-start.14 = (f32[2880]{0:T(1024)S(1)}, f32[2880]{0:T(1024)}, u32[]{:S(2)}) copy-start(f32[2880]{0:T(1024)} %param.33) | copy-start | bytes 34564
  305.9 61.4 %all-to-all-start = ((bf16[32,20,2880]{2,1,0:T(8,128)(2,1)}), bf16[32,20,2880]{2,1,0:T(8,128)(2,1)}, u32[]{:S(2)}, u32[]{:S(2)}) async-start(bf16[32,20,2880]{2,1,0:T(8,128)(2,1)} %copy.105), calls=%async_computation | async-start | bytes 9043968 | tf_op jit(solution)/shard_map/all_to_all | solution.py:258
  315.0 107.6 %collective-permute-start.7 = (bf16[192,2880]{1,0:T(8,128)(2,1)}, bf16[192,2880]{1,0:T(8,128)(2,1)}, u32[]{:S(2)}, u32[]{:S(2)}) collective-permute-start(bf16[192,2880]{1,0:T(8,128)(2,1)} %copy.111), channel_id=1, source_target_pairs={{0,96},{32,0},{64,32},{96,64},{1,97},{33,1},{65,33},{97,65},{2,98}... | collective-permute-start | bytes 3317768 | tf_op jit(solution)/shard_map/ppermute | solution.py:75
  320.6 61.7 %collective-permute-start.4 = (bf16[384,2880]{0,1:T(8,128)(2,1)}, bf16[384,2880]{0,1:T(8,128)(2,1)}, u32[]{:S(2)}, u32[]{:S(2)}) collective-permute-start(bf16[384,2880]{0,1:T(8,128)(2,1)} %slice_bitcast_fusion.5), channel_id=1, source_target_pairs={{0,32},{32,64},{64,96},{96,0},{1,33},{33,65},{65,97},{97,1},{2,34}... | collective-permute-start | bytes 6635528 | tf_op jit(solution)/shard_map/ppermute | solution.py:74
  323.9 80.7 %collective-permute-start.5 = (bf16[384,2880]{0,1:T(8,128)(2,1)}, bf16[384,2880]{0,1:T(8,128)(2,1)}, u32[]{:S(2)}, u32[]{:S(2)}) collective-permute-start(bf16[384,2880]{0,1:T(8,128)(2,1)} %slice_bitcast_fusion.4), channel_id=1, source_target_pairs={{0,96},{32,0},{64,32},{96,64},{1,97},{33,1},{65,33},{97,65},{2,98}... | collective-permute-start | bytes 6635528 | tf_op jit(solution)/shard_map/ppermute | solution.py:75
  329.8 95.2 %collective-permute-start.6 = (bf16[192,2880]{1,0:T(8,128)(2,1)}, bf16[192,2880]{1,0:T(8,128)(2,1)S(1)}, u32[]{:S(2)}, u32[]{:S(2)}) collective-permute-start(bf16[192,2880]{1,0:T(8,128)(2,1)} %copy.109), channel_id=1, source_target_pairs={{0,32},{32,64},{64,96},{96,0},{1,33},{33,65},{65,97},{97,1},{2,34}... | collective-permute-start | bytes 3317768 | tf_op jit(solution)/shard_map/ppermute | solution.py:74
  367.3 10.5 %slice-start.2 = ((s8[4423680]{0:T(1024)(128)(4,1)}), s8[4194304]{0:T(1024)(128)(4,1)S(1)}, s32[]{:S(2)}) async-start(s8[4423680]{0:T(1024)(128)(4,1)} %bitcast.204), calls=%async_computation.6 | async-start | bytes 8388608
  372.6 5.2 %slice-start.3 = ((s8[4423680]{0:T(1024)(128)(4,1)}), s8[229376]{0:T(1024)(128)(4,1)S(1)}, s32[]{:S(2)}) async-start(s8[4423680]{0:T(1024)(128)(4,1)} %bitcast.204), calls=%async_computation.7 | async-start | bytes 458752
  414.2 4.2 copy-start.19
  430.3 61.8 %copy-start.4 = (f32[128,32,20]{0,1,2:T(8,128)S(1)}, f32[128,32,20]{0,1,2:T(8,128)}, u32[]{:S(2)}) copy-start(f32[128,32,20]{0,1,2:T(8,128)} %get-tuple-element.18) | copy-start | bytes 983044
  (4 other events, 4.1 us)
Sparse Core Ops, SparseCore 0:
  14.1 151.6 all-gather.5
  188.1 47.5 all-gather.3

commit v4 on v3

--- a/solution.py
+++ b/solution.py
@@ -48,12 +48,6 @@
 def spread(adapter_selector, low_part):
     joined = adapter_selector[:, :, None] * low_part.astype(jnp.float32)[:, None, :]
     return joined.reshape(joined.shape[0], -1).astype(jnp.bfloat16)
-
-
-def expert_hidden(rows_in, gate_up):
-    gate_out = multiply_rows(rows_in, gate_up[:, 0, :])
-    up_out = multiply_rows(rows_in, gate_up[:, 1, :])
-    return (jax.nn.silu(gate_out) * up_out).astype(jnp.bfloat16)
 
 
 def gather_expert_blocks(gate_up_local, down_local, anchor=None):
@@ -138,9 +132,7 @@
         offset += width
     all_down, all_up_query, all_up_keyval, all_o_down, all_o_up = factors
     gate_up_local = jnp.transpose(expert_gate_up_weight[0], (1, 0, 2))
-    gate_up_local, down_local, _ = lax.optimization_barrier(
-        (gate_up_local, expert_down_weight[0], all_factors)
-    )
+    down_local = expert_down_weight[0]
     adapter_table = all_down.shape[0]
     adapter_selector = (
         adapter_of[:, None] == jnp.arange(adapter_table, dtype=jnp.int32)[None, :]
@@ -220,7 +212,7 @@
         .reshape(tok_rows, q_width)
         .astype(jnp.bfloat16)
     )
-    attended, expert_blocks = gather_expert_blocks(gate_up_local, down_local, attended)
+    _, expert_blocks = gather_expert_blocks(gate_up_local, down_local)
     o_low = select_adapter(
         multiply_rows(attended, all_o_down.reshape(adapter_table * ADAPTER_RANK, q_width)),
         adapter_selector,
@@ -306,6 +298,7 @@
         P(("dp", "expert"), None),
         P(("dp", "expert"), None),
     )
+
     return jax.shard_map(
         shards, mesh=mesh, in_specs=placed, out_specs=P(("dp", "expert"), None), check_vma=False
     )

time: 513 us -> 524 us (1.021)
  waiting for transfers between devices: 189 us -> 200 us
    ppermute x2, waiting for transfers between devices: 0.01 us -> 12.4 us  [gather_expert_blocks(): lax.ppermute((gate_up_prev[0], down_prev[:half]), 'dp', forward)]
    unnamed x58 -> x60, local copies, waits for them, and re-layouts: 14.4 us -> 15.9 us
  transfers between devices with their start and end apart: 11 -> 11, of which waited for: 3 -> 4; matrix products, arithmetic and copies ran while one was open for 33% -> 35% of each run, Pallas kernels for 0% -> 0%
where the time goes in v4:
time: 524 us; the launch traced here: 519 us
  waiting for transfers between devices  200 us (38%)
  matrix products  114 us (22%)
  blocking collectives  88.2 us (17%)
  local copies, waits for them, and re-layouts  66.4 us (13%)
  other arithmetic  20.1 us (4%)
  starting transfers between devices  15.4 us (3%)
  between operations  14.3 us (3%)
    all_gather x1, waiting for transfers between devices, shards(): all_factors = lax.all_gather(joined_factors, 'dp', axis=0, tiled=True)  116 us
    all_to_all x1, blocking collectives, shards(): lax.all_to_all(expert_rows, 'expert', split_axis=0, concat_axis=0, tiled=...  62.9 us
    all_to_all x1, waiting for transfers between devices, shards(): lax.all_to_all(dispatch, 'expert', split_axis=0, concat_axis=0, tiled=True)  37.5 us
    all_gather x1, waiting for transfers between devices, shards(): lax.all_gather(jnp.concatenate([key_rows, value_rows], axis=1), 'expert',...  34.4 us
    all_gather x1, blocking collectives, shards(): row_ids = lax.all_gather(prompt_number, 'expert', axis=1, tiled=True)[0]  25.3 us
    dot_general x4, matrix products, shards(): jnp.einsum('esd,fd->esf', arrived, up_w, preferred_element_type=jnp.float32)  22.5 us
    dot_general x4, matrix products, shards(): jnp.einsum('esd,fd->esf', arrived, gate_w, preferred_element_type=jnp.flo...  21.2 us
    dot_general x5, matrix products, shards(): jnp.einsum('esf,fd->esd', activation[:, :, offset:offset + down_w.shape[0...  18.5 us
  transfers between devices with their start and end apart: 11, of which 4 were waited for; matrix products, arithmetic and copies ran while one was open for 35% of the time, Pallas kernels for 0%

profile of v4, /device:TPU:1, one launch (start us, length us, event | category | flops | bytes accessed | tf_op | source)
XLA Modules:
  0.0 518.9 jit_solution(16205468705822345353)
XLA Ops:
  19.2 25.3 %all_gather.9 = s32[1,4096]{1,0:T(1,128)S(1)} all-gather(s32[1,128]{1,0:T(1,128)S(1)} %copy-done.17), channel_id=1, replica_groups=mesh['dp'=4,'expert'=32] {'expert'}, dimensions={1}, use_global_device_ids=true | all-gather | bytes 16896 | tf_op jit(solution)/shard_map/all_gather | solution.py:106
  49.7 116.0 %all-gather.6.cloned.1.call-done = bf16[4,4,258048]{2,1,0:T(4,128)(2,1)} async-done(((bf16[1,4,258048]{2,1,0:T(4,128)(2,1)}), bf16[4,4,258048]{2,1,0:T(4,128)(2,1)}) %all-gather.6.cloned.1.call-update) | async-done | bytes 8257552 | tf_op jit(solution)/shard_map/all_gather | solution.py:124
  165.7 6.4 %reshape.378 = bf16[16,258048]{1,0:T(8,128)(2,1)} reshape(bf16[4,4,258048]{2,1,0:T(4,128)(2,1)} %all-gather.6.cloned.1.call-done) | data formatting | bytes 16515072
  172.1 3.8 slice.114
  175.9 6.8 %dot_general.78 = bf16[16,48,2880]{2,1,0:T(8,128)(2,1)} reshape(bf16[16,138240]{1,0:T(8,128)(2,1)} %slice.114) | data formatting | bytes 8847360 | tf_op jit(solution)/shard_map/dot_general | solution.py:38
  182.7 3.8 fusion.54
  201.2 34.4 %all-gather.4.cloned.1.call-done = bf16[4096,512]{1,0:T(8,128)(2,1)} async-done(((bf16[128,512]{1,0:T(8,128)(2,1)}), bf16[4096,512]{1,0:T(8,128)(2,1)}) %all-gather.4.cloned.1.call-update) | async-done | bytes 4194320 | tf_op jit(solution)/shard_map/all_gather | solution.py:177
  235.7 3.8 fusion.99
  239.5 4.2 copy.71
  243.7 18.3 %fusion.101 = (f32[4,8,128]{2,1,0:T(8,128)S(1)}, f32[4,8,128,2176]{2,3,1,0:T(8,128)}) fusion(bf16[128,4,8,32]{0,3,2,1:T(8,128)(2,1)S(1)} %bitcast.181, bf16[128,4,8,32]{0,3,2,1:T(8,128)(2,1)S(1)} %bitcast.180, bf16[4096,4,64]{0,2,1:T(8,128)(2,1)} %bitcast.175, s32[]{:T(128)S(6)} %min.4, pred[128,2176]{0,1:T(8,128)(4,1)S(1)} %compare_and_fusion), kind=kOutput, calls=%fused_computation.160 | convolution fusion | flops 1168633856 | bytes 37584900 | tf_op jit(solution)/shard_map/tkgd,nkd->kgtn/dot_general | solution.py:193
  262.1 13.6 %fusion = f32[4,8,128]{2,1,0:T(8,128)S(1)} fusion(f32[4,8,128,2176]{2,3,1,0:T(8,128)} %get-tuple-element.27, f32[4,8,128]{2,1,0:T(8,128)S(1)} %broadcast_maximum_fusion), kind=kLoop, calls=%fused_computation.2 | loop fusion | flops 17821696 | bytes 35684352 | tf_op jit(solution)/shard_map/reduce_sum | solution.py:203
  278.8 14.3 %fusion.51 = bf16[128,4,8,64]{0,3,2,1:T(8,128)(2,1)S(1)} fusion(f32[4,8,128,2176]{2,3,1,0:T(8,128)} %get-tuple-element.27, f32[4,8,128]{2,1,0:T(8,128)S(1)} %broadcast_maximum_fusion, bf16[4096,4,64]{0,2,1:T(8,128)(2,1)} %bitcast.176, s32[]{:T(128)S(6)} %min.4, f32[128,4,8]{0,2,1:T(8,128)S(1)} %get-tuple-element.20, f32[128,4,8]{0,2,1:T(8,128)S(1)} %get-tuple-element.19), kind=kOutput, calls=%fused_computation.60 | convolution fusion | flops 1159462912 | bytes 37339140 | tf_op jit(solution)/shard_map/kgtn,nkd->kgtd/dot_general | solution.py:204
  293.1 6.4 %fusion.102 = f32[128,2880]{0,1:T(8,128)S(1)} fusion(bf16[2048,2880]{0,1:T(8,128)(2,1)} %param.32, bf16[128,2048]{0,1:T(8,128)(2,1)S(1)} %bitcast.187), kind=kOutput, calls=%fused_computation.161 | convolution fusion | flops 1509949440 | bytes 13795328 | tf_op jit(solution)/shard_map/dot_general | solution.py:221
  303.3 3.3 copy.80
  306.5 5.4 %all-to-all-start = ((bf16[32,20,2880]{2,1,0:T(8,128)(2,1)}), bf16[32,20,2880]{2,1,0:T(8,128)(2,1)}, u32[]{:S(2)}, u32[]{:S(2)}) async-start(bf16[32,20,2880]{2,1,0:T(8,128)(2,1)} %copy.80), calls=%async_computation | async-start | bytes 9043968 | tf_op jit(solution)/shard_map/all_to_all | solution.py:250
  321.2 3.2 slice_bitcast_fusion.9
  324.6 3.3 slice_bitcast_fusion.8
  330.4 37.5 %all-to-all-done = bf16[32,20,2880]{2,1,0:T(8,128)(2,1)} async-done(((bf16[32,20,2880]{2,1,0:T(8,128)(2,1)}), bf16[32,20,2880]{2,1,0:T(8,128)(2,1)}, u32[]{:S(2)}, u32[]{:S(2)}) %all-to-all-start) | async-done | bytes 3686432 | tf_op jit(solution)/shard_map/all_to_all | solution.py:250
  367.9 5.2 fusion.22
  373.1 5.3 %fusion.31 = f32[32,20,384]{2,1,0:T(8,128)S(1)} fusion(bf16[32,20,2880]{2,1,0:T(8,128)(2,1)} %all-to-all-done, bf16[2,384,2880]{1,2,0:T(8,128)(2,1)} %collective-permute-done), kind=kOutput, calls=%fused_computation.38 | convolution fusion | flops 1415577600 | bytes 7716864 | tf_op jit(solution)/shard_map/esd,fd->esf/dot_general | solution.py:253
  378.4 5.2 %fusion.19 = f32[32,20,384]{2,1,0:T(8,128)S(1)} fusion(bf16[32,20,2880]{2,1,0:T(8,128)(2,1)} %all-to-all-done, bf16[2,384,2880]{1,2,0:T(8,128)(2,1)} %collective-permute-done.2), kind=kOutput, calls=%fused_computation.23 | convolution fusion | flops 1415577600 | bytes 7716864 | tf_op jit(solution)/shard_map/esd,fd->esf/dot_general | solution.py:253
  383.6 12.4 %collective-permute-done.4 = bf16[384,2880]{0,1:T(8,128)(2,1)} collective-permute-done((bf16[384,2880]{0,1:T(8,128)(2,1)}, bf16[384,2880]{0,1:T(8,128)(2,1)}, u32[]{:S(2)}, u32[]{:S(2)}) %collective-permute-start.4) | collective-permute-done | bytes 2211872 | tf_op jit(solution)/shard_map/ppermute | solution.py:68
  396.0 5.6 %fusion.25 = f32[32,20,384]{2,1,0:T(8,128)S(1)} fusion(bf16[32,20,2880]{2,1,0:T(8,128)(2,1)} %all-to-all-done, bf16[384,2880]{0,1:T(8,128)(2,1)} %collective-permute-done.4), kind=kOutput, calls=%fused_computation.32 | convolution fusion | flops 1415577600 | bytes 6881280 | tf_op jit(solution)/shard_map/esd,fd->esf/dot_general | solution.py:253
  401.6 5.1 fusion.46
  406.7 5.8 %multiply_convert_fusion.3 = bf16[32,20,384]{2,1,0:T(8,128)(2,1)S(1)} fusion(f32[32,20,384]{2,1,0:T(8,128)S(1)} %fusion.31, bf16[32,20,2880]{2,1,0:T(8,128)(2,1)} %all-to-all-done, bf16[2,384,2880]{1,2,0:T(8,128)(2,1)} %collective-permute-done), kind=kOutput, calls=%fused_computation.64 | convolution fusion | flops 1417052160 | bytes 8208384 | tf_op jit(solution)/shard_map/esd,fd->esf/dot_general | solution.py:254
  412.5 5.8 %multiply_convert_fusion.2 = bf16[32,20,384]{2,1,0:T(8,128)(2,1)S(1)} fusion(f32[32,20,384]{2,1,0:T(8,128)S(1)} %fusion.19, bf16[32,20,2880]{2,1,0:T(8,128)(2,1)} %all-to-all-done, bf16[2,384,2880]{1,2,0:T(8,128)(2,1)} %collective-permute-done.2), kind=kOutput, calls=%fused_computation.63 | convolution fusion | flops 1417052160 | bytes 8208384 | tf_op jit(solution)/shard_map/esd,fd->esf/dot_general | solution.py:254
  418.3 5.9 %multiply_convert_fusion.1 = bf16[32,20,384]{2,1,0:T(8,128)(2,1)S(1)} fusion(f32[32,20,384]{2,1,0:T(8,128)S(1)} %fusion.25, bf16[32,20,2880]{2,1,0:T(8,128)(2,1)} %all-to-all-done, bf16[384,2880]{0,1:T(8,128)(2,1)} %collective-permute-done.5), kind=kOutput, calls=%fused_computation.62 | convolution fusion | flops 1417052160 | bytes 7372800 | tf_op jit(solution)/shard_map/esd,fd->esf/dot_general | solution.py:254
  426.4 3.8 convolution_convert_fusion.1
  430.4 5.8 %convolution_convert_fusion = bf16[32,20,2880]{2,0,1:T(8,128)(2,1)} fusion(bf16[384,2880]{0,1:T(8,128)(2,1)} %collective-permute-done.3, bf16[32,20,384]{2,1,0:T(8,128)(2,1)S(1)} %multiply_convert_fusion.2), kind=kOutput, calls=%fused_computation.8 | convolution fusion | flops 1417420800 | bytes 6389760 | tf_op jit(solution)/shard_map/esf,fd->esd/dot_general | solution.py:259
  438.7 4.2 add_convert_fusion
  444.0 62.9 %all_to_all.10 = bf16[32,20,2880]{2,1,0:T(8,128)(2,1)S(1)} all-to-all(bf16[32,20,2880]{2,1,0:T(8,128)(2,1)S(1)} %copy.88), channel_id=1, replica_groups=mesh['dp'=4,'expert'=32] {'expert'}, dimensions={0} | all-to-all | bytes 7372800 | tf_op jit(solution)/shard_map/all_to_all | solution.py:268
  507.0 4.9 fusion.16
  (148 shorter events, 57.1 us)
Async XLA Ops:
  6.5 159.2 %all-gather.6.cloned.1.call-start = ((), (), s32[]{:S(2)}) async-start(), calls=%async_computation.3 | async-start | bytes 10321920 | tf_op jit(solution)/shard_map/all_gather | solution.py:124
  10.7 8.2 %copy-start.16 = (s32[128,4]{0,1:T(4,128)S(1)}, s32[128,4]{0,1:T(4,128)}, u32[]{:S(2)}) copy-start(s32[128,4]{0,1:T(4,128)} %param.36) | copy-start | bytes 6148
  12.1 7.1 %copy-start.17 = (s32[1,128]{1,0:T(1,128)S(1)}, s32[1,128]{1,0:T(1,128)}, u32[]{:S(2)}) copy-start(s32[1,128]{1,0:T(1,128)} %param.23) | copy-start | bytes 1540
  12.2 35.3 %copy-start.19 = (s32[1,16]{1,0:T(1,128)S(1)}, s32[1,16]{1,0:T(1,128)}, u32[]{:S(2)}) copy-start(s32[1,16]{1,0:T(1,128)} %param.24) | copy-start | bytes 196
  12.2 35.4 %copy-start.2 = (bf16[128,2880]{0,1:T(8,128)(2,1)S(1)}, bf16[128,2880]{0,1:T(8,128)(2,1)}, u32[]{:S(2)}) copy-start(bf16[128,2880]{0,1:T(8,128)(2,1)} %param.19) | copy-start | bytes 2211844
  12.6 1.3 copy-start.1
  13.9 221.7 %all-gather.4.cloned.1.call-start = ((), (), s32[]{:S(2)}) async-start(), calls=%async_computation.2 | async-start | bytes 4325376 | tf_op jit(solution)/shard_map/all_gather | solution.py:177
  14.0 307.2 %collective-permute-start = (bf16[2,384,2880]{1,2,0:T(8,128)(2,1)}, bf16[2,384,2880]{1,2,0:T(8,128)(2,1)}, u32[]{:S(2)}, u32[]{:S(2)}) collective-permute-start(bf16[2,384,2880]{1,2,0:T(8,128)(2,1)} %bitcast.202), channel_id=1, source_target_pairs={{0,32},{32,64},{64,96},{96,0},{1,33},{33,65},{65,97},{97,1},{2,34}... | collective-permute-start | bytes 13271048 | tf_op jit(solution)/shard_map/ppermute | solution.py:61
  16.1 308.6 %collective-permute-start.2 = (bf16[2,384,2880]{1,2,0:T(8,128)(2,1)}, bf16[2,384,2880]{1,2,0:T(8,128)(2,1)}, u32[]{:S(2)}, u32[]{:S(2)}) collective-permute-start(bf16[2,384,2880]{1,2,0:T(8,128)(2,1)} %bitcast.203), channel_id=1, source_target_pairs={{0,96},{32,0},{64,32},{96,64},{1,97},{33,1},{65,33},{97,65},{2,98}... | collective-permute-start | bytes 13271048 | tf_op jit(solution)/shard_map/ppermute | solution.py:62
  17.4 294.5 %collective-permute-start.3 = (bf16[384,2880]{0,1:T(8,128)(2,1)}, bf16[384,2880]{0,1:T(8,128)(2,1)}, u32[]{:S(2)}, u32[]{:S(2)}) collective-permute-start(bf16[384,2880]{0,1:T(8,128)(2,1)} %bitcast.208), channel_id=1, source_target_pairs={{0,96},{32,0},{64,32},{96,64},{1,97},{33,1},{65,33},{97,65},{2,98}... | collective-permute-start | bytes 6635528 | tf_op jit(solution)/shard_map/ppermute | solution.py:62
  18.8 299.2 %collective-permute-start.1 = (bf16[384,2880]{0,1:T(8,128)(2,1)}, bf16[384,2880]{0,1:T(8,128)(2,1)}, u32[]{:S(2)}, u32[]{:S(2)}) collective-permute-start(bf16[384,2880]{0,1:T(8,128)(2,1)} %bitcast.209), channel_id=1, source_target_pairs={{0,32},{32,64},{64,96},{96,0},{1,33},{33,65},{65,97},{97,1},{2,34}... | collective-permute-start | bytes 6635528 | tf_op jit(solution)/shard_map/ppermute | solution.py:61
  175.9 6.8 %copy-start.21 = (f32[2880]{0:T(1024)S(1)}, f32[2880]{0:T(1024)}, u32[]{:S(2)}) copy-start(f32[2880]{0:T(1024)} %param.26) | copy-start | bytes 34564
  182.7 3.8 slice-start
  182.7 3.9 copy-start.14
  182.7 4.4 copy-start.12
  186.5 1.5 copy-start.18
  189.0 3.3 copy-start.9
  193.6 4.5 slice-start.1
  239.5 4.2 copy-start.5
  239.5 4.2 copy-start.6
  293.1 6.4 %copy-start.7 = (bf16[2,8,16,2048]{3,2,1,0:T(8,128)(2,1)S(1)}, bf16[2,8,16,2048]{3,2,1,0:T(8,128)(2,1)}, u32[]{:S(2)}) copy-start(bf16[2,8,16,2048]{3,2,1,0:T(8,128)(2,1)} %copy.100) | copy-start | bytes 3145732
  299.5 1.4 copy-start
  299.6 1.6 copy-start.3
  306.5 61.4 %all-to-all-start = ((bf16[32,20,2880]{2,1,0:T(8,128)(2,1)}), bf16[32,20,2880]{2,1,0:T(8,128)(2,1)}, u32[]{:S(2)}, u32[]{:S(2)}) async-start(bf16[32,20,2880]{2,1,0:T(8,128)(2,1)} %copy.80), calls=%async_computation | async-start | bytes 9043968 | tf_op jit(solution)/shard_map/all_to_all | solution.py:250
  315.6 120.7 %collective-permute-start.7 = (bf16[192,2880]{1,0:T(8,128)(2,1)}, bf16[192,2880]{1,0:T(8,128)(2,1)}, u32[]{:S(2)}, u32[]{:S(2)}) collective-permute-start(bf16[192,2880]{1,0:T(8,128)(2,1)} %copy.86), channel_id=1, source_target_pairs={{0,96},{32,0},{64,32},{96,64},{1,97},{33,1},{65,33},{97,65},{2,98}... | collective-permute-start | bytes 3317768 | tf_op jit(solution)/shard_map/ppermute | solution.py:69
  321.2 117.5 %collective-permute-start.6 = (bf16[192,2880]{1,0:T(8,128)(2,1)}, bf16[192,2880]{1,0:T(8,128)(2,1)S(1)}, u32[]{:S(2)}, u32[]{:S(2)}) collective-permute-start(bf16[192,2880]{1,0:T(8,128)(2,1)} %copy.84), channel_id=1, source_target_pairs={{0,32},{32,64},{64,96},{96,0},{1,33},{33,65},{65,97},{97,1},{2,34}... | collective-permute-start | bytes 3317768 | tf_op jit(solution)/shard_map/ppermute | solution.py:68
  324.4 71.6 %collective-permute-start.4 = (bf16[384,2880]{0,1:T(8,128)(2,1)}, bf16[384,2880]{0,1:T(8,128)(2,1)}, u32[]{:S(2)}, u32[]{:S(2)}) collective-permute-start(bf16[384,2880]{0,1:T(8,128)(2,1)} %slice_bitcast_fusion.9), channel_id=1, source_target_pairs={{0,32},{32,64},{64,96},{96,0},{1,33},{33,65},{65,97},{97,1},{2,34}... | collective-permute-start | bytes 6635528 | tf_op jit(solution)/shard_map/ppermute | solution.py:68
  327.9 90.3 %collective-permute-start.5 = (bf16[384,2880]{0,1:T(8,128)(2,1)}, bf16[384,2880]{0,1:T(8,128)(2,1)}, u32[]{:S(2)}, u32[]{:S(2)}) collective-permute-start(bf16[384,2880]{0,1:T(8,128)(2,1)} %slice_bitcast_fusion.8), channel_id=1, source_target_pairs={{0,96},{32,0},{64,32},{96,64},{1,97},{33,1},{65,33},{97,65},{2,98}... | collective-permute-start | bytes 6635528 | tf_op jit(solution)/shard_map/ppermute | solution.py:69
  373.1 28.5 %slice-start.2 = ((s8[4423680]{0:T(1024)(128)(4,1)}), s8[4194304]{0:T(1024)(128)(4,1)S(1)}, s32[]{:S(2)}) async-start(s8[4423680]{0:T(1024)(128)(4,1)} %bitcast.205), calls=%async_computation.6 | async-start | bytes 8388608
  378.4 23.2 %slice-start.3 = ((s8[4423680]{0:T(1024)(128)(4,1)}), s8[229376]{0:T(1024)(128)(4,1)S(1)}, s32[]{:S(2)}) async-start(s8[4423680]{0:T(1024)(128)(4,1)} %bitcast.205), calls=%async_computation.7 | async-start | bytes 458752
  418.3 5.9 %copy-start.20 = (bf16[1,384,2880]{1,2,0:T(8,128)(2,1)S(1)}, bf16[1,384,2880]{1,2,0:T(8,128)(2,1)}, u32[]{:S(2)}) copy-start(bf16[1,384,2880]{1,2,0:T(8,128)(2,1)} %param.35) | copy-start | bytes 6635524
  444.0 62.9 %copy-start.4 = (f32[128,32,20]{0,1,2:T(8,128)S(1)}, f32[128,32,20]{0,1,2:T(8,128)}, u32[]{:S(2)}) copy-start(f32[128,32,20]{0,1,2:T(8,128)} %get-tuple-element.6) | copy-start | bytes 983044
  (5 other events, 4.6 us)
Sparse Core Ops, SparseCore 0:
  14.1 151.6 all-gather.5
  188.1 47.5 all-gather.3

commit v5 on v4

--- a/solution.py
+++ b/solution.py
@@ -121,13 +121,14 @@
     )
     local_count = adapter_down_factors.shape[0]
     joined_factors = jnp.concatenate([f.reshape(local_count, -1) for f in local_factors], axis=1)
-    all_factors = lax.all_gather(joined_factors, "dp", axis=0, tiled=True)
+    all_factors = lax.all_gather(joined_factors, "dp", axis=0, tiled=False)
+    adapter_total = all_factors.shape[0] * local_count
     factors = []
     offset = 0
     for f in local_factors:
         width = f.shape[1] * f.shape[2]
         factors.append(
-            all_factors[:, offset : offset + width].reshape(all_factors.shape[0], f.shape[1], f.shape[2])
+            all_factors[:, :, offset : offset + width].reshape(adapter_total, f.shape[1], f.shape[2])
         )
         offset += width
     all_down, all_up_query, all_up_keyval, all_o_down, all_o_up = factors

time: 524 us -> 519 us (level)
    unnamed x60 -> x57, local copies, waits for them, and re-layouts: 15.9 us -> 6.84 us
  transfers between devices with their start and end apart: 11 -> 11, of which waited for: 4 -> 4; matrix products, arithmetic and copies ran while one was open for 35% -> 34% of each run, Pallas kernels for 0% -> 0%
where the time goes in v5:
time: 519 us; the launch traced here: 515 us
  waiting for transfers between devices  202 us (39%)
  matrix products  113 us (22%)
  blocking collectives  87.9 us (17%)
  local copies, waits for them, and re-layouts  62.1 us (12%)
  other arithmetic  20.5 us (4%)
  starting transfers between devices  15.4 us (3%)
  between operations  14.3 us (3%)
    all_gather x1, waiting for transfers between devices, shards(): all_factors = lax.all_gather(joined_factors, 'dp', axis=0, tiled=False)  116 us
    all_to_all x1, blocking collectives, shards(): lax.all_to_all(expert_rows, 'expert', split_axis=0, concat_axis=0, tiled=...  62.9 us
    all_to_all x1, waiting for transfers between devices, shards(): lax.all_to_all(dispatch, 'expert', split_axis=0, concat_axis=0, tiled=True)  37.5 us
    all_gather x1, waiting for transfers between devices, shards(): lax.all_gather(jnp.concatenate([key_rows, value_rows], axis=1), 'expert',...  35.6 us
    all_gather x1, blocking collectives, shards(): row_ids = lax.all_gather(prompt_number, 'expert', axis=1, tiled=True)[0]  24.9 us
    dot_general x4, matrix products, shards(): jnp.einsum('esd,fd->esf', arrived, up_w, preferred_element_type=jnp.float32)  22.5 us
    dot_general x4, matrix products, shards(): jnp.einsum('esd,fd->esf', arrived, gate_w, preferred_element_type=jnp.flo...  21 us
    dot_general x5, matrix products, shards(): jnp.einsum('esf,fd->esd', activation[:, :, offset:offset + down_w.shape[0...  18.5 us
  transfers between devices with their start and end apart: 11, of which 4 were waited for; matrix products, arithmetic and copies ran while one was open for 34% of the time, Pallas kernels for 0%

profile of v5, /device:TPU:1, one launch (start us, length us, event | category | flops | bytes accessed | tf_op | source)
XLA Modules:
  0.0 514.6 jit_solution(12144594424653507398)
XLA Ops:
  19.3 24.9 %all_gather.12 = s32[1,4096]{1,0:T(1,128)S(1)} all-gather(s32[1,128]{1,0:T(1,128)S(1)} %copy-done.17), channel_id=1, replica_groups=mesh['dp'=4,'expert'=32] {'expert'}, dimensions={1}, use_global_device_ids=true | all-gather | bytes 16896 | tf_op jit(solution)/shard_map/all_gather | solution.py:106
  49.4 116.4 %all-gather.7.cloned.1.call-done = bf16[4,4,258048]{2,1,0:T(4,128)(2,1)} async-done(((bf16[1,4,258048]{2,1,0:T(4,128)(2,1)}), bf16[4,4,258048]{2,1,0:T(4,128)(2,1)}) %all-gather.7.cloned.1.call-update) | async-done | bytes 8257552 | tf_op jit(solution)/shard_map/all_gather | solution.py:124
  165.8 5.4 %slice.114 = bf16[4,4,138240]{2,1,0:T(4,128)(2,1)} slice(bf16[4,4,258048]{2,1,0:T(4,128)(2,1)} %all-gather.7.cloned.1.call-done), slice={[0:4], [0:4], [0:138240]} | slice | bytes 8847360 | tf_op jit(solution)/shard_map/slice | solution.py:131
  171.2 7.1 %dot_general.78 = bf16[16,48,2880]{2,1,0:T(8,128)(2,1)} reshape(bf16[4,4,138240]{2,1,0:T(4,128)(2,1)} %slice.114) | data formatting | bytes 8847360 | tf_op jit(solution)/shard_map/dot_general | solution.py:38
  178.3 3.8 fusion.54
  184.8 3.3 fusion.98
  195.8 35.6 %all-gather.5.cloned.1.call-done = bf16[4096,512]{1,0:T(8,128)(2,1)} async-done(((bf16[128,512]{1,0:T(8,128)(2,1)}), bf16[4096,512]{1,0:T(8,128)(2,1)}) %all-gather.5.cloned.1.call-update) | async-done | bytes 4194320 | tf_op jit(solution)/shard_map/all_gather | solution.py:178
  231.5 3.8 fusion.99
  235.3 4.2 copy.71
  239.5 18.1 %fusion.101 = (f32[4,8,128]{2,1,0:T(8,128)S(1)}, f32[4,8,128,2176]{2,3,1,0:T(8,128)}) fusion(bf16[128,4,8,32]{0,3,2,1:T(8,128)(2,1)S(1)} %bitcast.175, bf16[128,4,8,32]{0,3,2,1:T(8,128)(2,1)S(1)} %bitcast.174, bf16[4096,4,64]{0,2,1:T(8,128)(2,1)} %bitcast.170, s32[]{:T(128)S(6)} %min.4, pred[128,2176]{0,1:T(8,128)(4,1)S(1)} %compare_and_fusion), kind=kOutput, calls=%fused_computation.160 | convolution fusion | flops 1168633856 | bytes 37584900 | tf_op jit(solution)/shard_map/tkgd,nkd->kgtn/dot_general | solution.py:194
  257.7 14.0 %fusion = f32[4,8,128]{2,1,0:T(8,128)S(1)} fusion(f32[4,8,128,2176]{2,3,1,0:T(8,128)} %get-tuple-element.27, f32[4,8,128]{2,1,0:T(8,128)S(1)} %broadcast_maximum_fusion), kind=kLoop, calls=%fused_computation.2 | loop fusion | flops 17821696 | bytes 35684352 | tf_op jit(solution)/shard_map/reduce_sum | solution.py:204
  274.8 14.3 %fusion.51 = bf16[128,4,8,64]{0,3,2,1:T(8,128)(2,1)S(1)} fusion(f32[4,8,128,2176]{2,3,1,0:T(8,128)} %get-tuple-element.27, f32[4,8,128]{2,1,0:T(8,128)S(1)} %broadcast_maximum_fusion, bf16[4096,4,64]{0,2,1:T(8,128)(2,1)} %bitcast.171, s32[]{:T(128)S(6)} %min.4, f32[128,4,8]{0,2,1:T(8,128)S(1)} %get-tuple-element.20, f32[128,4,8]{0,2,1:T(8,128)S(1)} %get-tuple-element.19), kind=kOutput, calls=%fused_computation.60 | convolution fusion | flops 1159462912 | bytes 37339140 | tf_op jit(solution)/shard_map/kgtn,nkd->kgtd/dot_general | solution.py:205
  289.1 6.2 %fusion.102 = f32[128,2880]{0,1:T(8,128)S(1)} fusion(bf16[2048,2880]{0,1:T(8,128)(2,1)} %param.32, bf16[128,2048]{0,1:T(8,128)(2,1)S(1)} %bitcast.178), kind=kOutput, calls=%fused_computation.161 | convolution fusion | flops 1509949440 | bytes 13795328 | tf_op jit(solution)/shard_map/dot_general | solution.py:222
  299.1 3.3 copy.80
  302.3 5.3 %all-to-all-start = ((bf16[32,20,2880]{2,1,0:T(8,128)(2,1)}), bf16[32,20,2880]{2,1,0:T(8,128)(2,1)}, u32[]{:S(2)}, u32[]{:S(2)}) async-start(bf16[32,20,2880]{2,1,0:T(8,128)(2,1)} %copy.80), calls=%async_computation | async-start | bytes 9043968 | tf_op jit(solution)/shard_map/all_to_all | solution.py:251
  317.0 3.2 slice_bitcast_fusion.9
  320.5 3.3 slice_bitcast_fusion.8
  326.2 37.5 %all-to-all-done = bf16[32,20,2880]{2,1,0:T(8,128)(2,1)} async-done(((bf16[32,20,2880]{2,1,0:T(8,128)(2,1)}), bf16[32,20,2880]{2,1,0:T(8,128)(2,1)}, u32[]{:S(2)}, u32[]{:S(2)}) %all-to-all-start) | async-done | bytes 3686432 | tf_op jit(solution)/shard_map/all_to_all | solution.py:251
  363.7 5.2 %fusion.22 = f32[32,20,384]{2,1,0:T(8,128)S(1)} fusion(bf16[32,20,2880]{2,1,0:T(8,128)(2,1)} %all-to-all-done, bf16[2,384,2880]{1,2,0:T(8,128)(2,1)} %bitcast.195), kind=kOutput, calls=%fused_computation.29 | convolution fusion | flops 1415577600 | bytes 7716864 | tf_op jit(solution)/shard_map/esd,fd->esf/dot_general | solution.py:254
  368.9 5.3 %fusion.31 = f32[32,20,384]{2,1,0:T(8,128)S(1)} fusion(bf16[32,20,2880]{2,1,0:T(8,128)(2,1)} %all-to-all-done, bf16[2,384,2880]{1,2,0:T(8,128)(2,1)} %collective-permute-done), kind=kOutput, calls=%fused_computation.38 | convolution fusion | flops 1415577600 | bytes 7716864 | tf_op jit(solution)/shard_map/esd,fd->esf/dot_general | solution.py:254
  374.2 5.2 %fusion.19 = f32[32,20,384]{2,1,0:T(8,128)S(1)} fusion(bf16[32,20,2880]{2,1,0:T(8,128)(2,1)} %all-to-all-done, bf16[2,384,2880]{1,2,0:T(8,128)(2,1)} %collective-permute-done.2), kind=kOutput, calls=%fused_computation.23 | convolution fusion | flops 1415577600 | bytes 7716864 | tf_op jit(solution)/shard_map/esd,fd->esf/dot_general | solution.py:254
  379.4 12.4 %collective-permute-done.4 = bf16[384,2880]{0,1:T(8,128)(2,1)} collective-permute-done((bf16[384,2880]{0,1:T(8,128)(2,1)}, bf16[384,2880]{0,1:T(8,128)(2,1)}, u32[]{:S(2)}, u32[]{:S(2)}) %collective-permute-start.4) | collective-permute-done | bytes 2211872 | tf_op jit(solution)/shard_map/ppermute | solution.py:68
  391.8 5.3 %fusion.25 = f32[32,20,384]{2,1,0:T(8,128)S(1)} fusion(bf16[32,20,2880]{2,1,0:T(8,128)(2,1)} %all-to-all-done, bf16[384,2880]{0,1:T(8,128)(2,1)} %collective-permute-done.4), kind=kOutput, calls=%fused_computation.32 | convolution fusion | flops 1415577600 | bytes 6881280 | tf_op jit(solution)/shard_map/esd,fd->esf/dot_general | solution.py:254
  397.2 5.1 fusion.46
  402.3 5.8 %multiply_convert_fusion.3 = bf16[32,20,384]{2,1,0:T(8,128)(2,1)S(1)} fusion(f32[32,20,384]{2,1,0:T(8,128)S(1)} %fusion.31, bf16[32,20,2880]{2,1,0:T(8,128)(2,1)} %all-to-all-done, bf16[2,384,2880]{1,2,0:T(8,128)(2,1)} %collective-permute-done), kind=kOutput, calls=%fused_computation.64 | convolution fusion | flops 1417052160 | bytes 8208384 | tf_op jit(solution)/shard_map/esd,fd->esf/dot_general | solution.py:255
  408.1 5.8 %multiply_convert_fusion.2 = bf16[32,20,384]{2,1,0:T(8,128)(2,1)S(1)} fusion(f32[32,20,384]{2,1,0:T(8,128)S(1)} %fusion.19, bf16[32,20,2880]{2,1,0:T(8,128)(2,1)} %all-to-all-done, bf16[2,384,2880]{1,2,0:T(8,128)(2,1)} %collective-permute-done.2), kind=kOutput, calls=%fused_computation.63 | convolution fusion | flops 1417052160 | bytes 8208384 | tf_op jit(solution)/shard_map/esd,fd->esf/dot_general | solution.py:255
  413.9 5.9 %multiply_convert_fusion.1 = bf16[32,20,384]{2,1,0:T(8,128)(2,1)S(1)} fusion(f32[32,20,384]{2,1,0:T(8,128)S(1)} %fusion.25, bf16[32,20,2880]{2,1,0:T(8,128)(2,1)} %all-to-all-done, bf16[384,2880]{0,1:T(8,128)(2,1)} %collective-permute-done.5), kind=kOutput, calls=%fused_computation.62 | convolution fusion | flops 1417052160 | bytes 7372800 | tf_op jit(solution)/shard_map/esd,fd->esf/dot_general | solution.py:255
  422.0 3.8 convolution_convert_fusion.1
  426.0 5.9 %convolution_convert_fusion = bf16[32,20,2880]{2,0,1:T(8,128)(2,1)} fusion(bf16[384,2880]{0,1:T(8,128)(2,1)} %collective-permute-done.3, bf16[32,20,384]{2,1,0:T(8,128)(2,1)S(1)} %multiply_convert_fusion.2), kind=kOutput, calls=%fused_computation.8 | convolution fusion | flops 1417420800 | bytes 6389760 | tf_op jit(solution)/shard_map/esf,fd->esd/dot_general | solution.py:260
  434.3 4.2 add_convert_fusion
  439.7 62.9 %all_to_all.10 = bf16[32,20,2880]{2,1,0:T(8,128)(2,1)S(1)} all-to-all(bf16[32,20,2880]{2,1,0:T(8,128)(2,1)S(1)} %copy.88), channel_id=1, replica_groups=mesh['dp'=4,'expert'=32] {'expert'}, dimensions={0} | all-to-all | bytes 7372800 | tf_op jit(solution)/shard_map/all_to_all | solution.py:269
  502.6 4.9 fusion.16
  (147 shorter events, 52.9 us)
Async XLA Ops:
  6.5 159.2 %all-gather.7.cloned.1.call-start = ((), (), s32[]{:S(2)}) async-start(), calls=%async_computation.3 | async-start | bytes 10321920 | tf_op jit(solution)/shard_map/all_gather | solution.py:124
  9.5 1.0 copy-start.11
  10.7 8.2 %copy-start.16 = (s32[128,4]{0,1:T(4,128)S(1)}, s32[128,4]{0,1:T(4,128)}, u32[]{:S(2)}) copy-start(s32[128,4]{0,1:T(4,128)} %param.36) | copy-start | bytes 6148
  12.1 7.2 %copy-start.17 = (s32[1,128]{1,0:T(1,128)S(1)}, s32[1,128]{1,0:T(1,128)}, u32[]{:S(2)}) copy-start(s32[1,128]{1,0:T(1,128)} %param.23) | copy-start | bytes 1540
  12.2 35.0 %copy-start.19 = (s32[1,16]{1,0:T(1,128)S(1)}, s32[1,16]{1,0:T(1,128)}, u32[]{:S(2)}) copy-start(s32[1,16]{1,0:T(1,128)} %param.24) | copy-start | bytes 196
  12.2 35.1 %copy-start.2 = (bf16[128,2880]{0,1:T(8,128)(2,1)S(1)}, bf16[128,2880]{0,1:T(8,128)(2,1)}, u32[]{:S(2)}) copy-start(bf16[128,2880]{0,1:T(8,128)(2,1)} %param.19) | copy-start | bytes 2211844
  12.6 1.4 copy-start.1
  14.0 217.5 %all-gather.5.cloned.1.call-start = ((), (), s32[]{:S(2)}) async-start(), calls=%async_computation.2 | async-start | bytes 4325376 | tf_op jit(solution)/shard_map/all_gather | solution.py:178
  14.0 303.0 %collective-permute-start = (bf16[2,384,2880]{1,2,0:T(8,128)(2,1)}, bf16[2,384,2880]{1,2,0:T(8,128)(2,1)}, u32[]{:S(2)}, u32[]{:S(2)}) collective-permute-start(bf16[2,384,2880]{1,2,0:T(8,128)(2,1)} %bitcast.193), channel_id=1, source_target_pairs={{0,32},{32,64},{64,96},{96,0},{1,33},{33,65},{65,97},{97,1},{2,34}... | collective-permute-start | bytes 13271048 | tf_op jit(solution)/shard_map/ppermute | solution.py:61
  16.1 304.3 %collective-permute-start.2 = (bf16[2,384,2880]{1,2,0:T(8,128)(2,1)}, bf16[2,384,2880]{1,2,0:T(8,128)(2,1)}, u32[]{:S(2)}, u32[]{:S(2)}) collective-permute-start(bf16[2,384,2880]{1,2,0:T(8,128)(2,1)} %bitcast.194), channel_id=1, source_target_pairs={{0,96},{32,0},{64,32},{96,64},{1,97},{33,1},{65,33},{97,65},{2,98}... | collective-permute-start | bytes 13271048 | tf_op jit(solution)/shard_map/ppermute | solution.py:62
  17.5 290.2 %collective-permute-start.3 = (bf16[384,2880]{0,1:T(8,128)(2,1)}, bf16[384,2880]{0,1:T(8,128)(2,1)}, u32[]{:S(2)}, u32[]{:S(2)}) collective-permute-start(bf16[384,2880]{0,1:T(8,128)(2,1)} %bitcast.199), channel_id=1, source_target_pairs={{0,96},{32,0},{64,32},{96,64},{1,97},{33,1},{65,33},{97,65},{2,98}... | collective-permute-start | bytes 6635528 | tf_op jit(solution)/shard_map/ppermute | solution.py:62
  18.9 295.0 %collective-permute-start.1 = (bf16[384,2880]{0,1:T(8,128)(2,1)}, bf16[384,2880]{0,1:T(8,128)(2,1)}, u32[]{:S(2)}, u32[]{:S(2)}) collective-permute-start(bf16[384,2880]{0,1:T(8,128)(2,1)} %bitcast.200), channel_id=1, source_target_pairs={{0,32},{32,64},{64,96},{96,0},{1,33},{33,65},{65,97},{97,1},{2,34}... | collective-permute-start | bytes 6635528 | tf_op jit(solution)/shard_map/ppermute | solution.py:61
  171.2 7.1 %copy-start.21 = (f32[2880]{0:T(1024)S(1)}, f32[2880]{0:T(1024)}, u32[]{:S(2)}) copy-start(f32[2880]{0:T(1024)} %param.26) | copy-start | bytes 34564
  178.3 3.8 slice-start
  178.3 4.0 copy-start.14
  182.1 1.7 copy-start.18
  184.8 4.2 copy-start.9
  189.6 2.7 slice-start.1
  235.3 4.2 copy-start.5
  235.3 4.2 copy-start.6
  289.1 6.2 %copy-start.7 = (bf16[16,16,2048]{2,1,0:T(8,128)(2,1)S(1)}, bf16[16,16,2048]{2,1,0:T(8,128)(2,1)}, u32[]{:S(2)}) copy-start(bf16[16,16,2048]{2,1,0:T(8,128)(2,1)} %dot_general.87) | copy-start | bytes 3145732
  295.4 1.4 copy-start
  295.4 1.6 copy-start.3
  302.3 61.4 %all-to-all-start = ((bf16[32,20,2880]{2,1,0:T(8,128)(2,1)}), bf16[32,20,2880]{2,1,0:T(8,128)(2,1)}, u32[]{:S(2)}, u32[]{:S(2)}) async-start(bf16[32,20,2880]{2,1,0:T(8,128)(2,1)} %copy.80), calls=%async_computation | async-start | bytes 9043968 | tf_op jit(solution)/shard_map/all_to_all | solution.py:251
  311.4 120.5 %collective-permute-start.7 = (bf16[192,2880]{1,0:T(8,128)(2,1)}, bf16[192,2880]{1,0:T(8,128)(2,1)}, u32[]{:S(2)}, u32[]{:S(2)}) collective-permute-start(bf16[192,2880]{1,0:T(8,128)(2,1)} %copy.86), channel_id=1, source_target_pairs={{0,96},{32,0},{64,32},{96,64},{1,97},{33,1},{65,33},{97,65},{2,98}... | collective-permute-start | bytes 3317768 | tf_op jit(solution)/shard_map/ppermute | solution.py:69
  317.0 117.3 %collective-permute-start.6 = (bf16[192,2880]{1,0:T(8,128)(2,1)}, bf16[192,2880]{1,0:T(8,128)(2,1)S(1)}, u32[]{:S(2)}, u32[]{:S(2)}) collective-permute-start(bf16[192,2880]{1,0:T(8,128)(2,1)} %copy.84), channel_id=1, source_target_pairs={{0,32},{32,64},{64,96},{96,0},{1,33},{33,65},{65,97},{97,1},{2,34}... | collective-permute-start | bytes 3317768 | tf_op jit(solution)/shard_map/ppermute | solution.py:68
  320.2 71.6 %collective-permute-start.4 = (bf16[384,2880]{0,1:T(8,128)(2,1)}, bf16[384,2880]{0,1:T(8,128)(2,1)}, u32[]{:S(2)}, u32[]{:S(2)}) collective-permute-start(bf16[384,2880]{0,1:T(8,128)(2,1)} %slice_bitcast_fusion.9), channel_id=1, source_target_pairs={{0,32},{32,64},{64,96},{96,0},{1,33},{33,65},{65,97},{97,1},{2,34}... | collective-permute-start | bytes 6635528 | tf_op jit(solution)/shard_map/ppermute | solution.py:68
  323.7 90.1 %collective-permute-start.5 = (bf16[384,2880]{0,1:T(8,128)(2,1)}, bf16[384,2880]{0,1:T(8,128)(2,1)}, u32[]{:S(2)}, u32[]{:S(2)}) collective-permute-start(bf16[384,2880]{0,1:T(8,128)(2,1)} %slice_bitcast_fusion.8), channel_id=1, source_target_pairs={{0,96},{32,0},{64,32},{96,64},{1,97},{33,1},{65,33},{97,65},{2,98}... | collective-permute-start | bytes 6635528 | tf_op jit(solution)/shard_map/ppermute | solution.py:69
  368.9 28.3 %slice-start.2 = ((s8[4423680]{0:T(1024)(128)(4,1)}), s8[4194304]{0:T(1024)(128)(4,1)S(1)}, s32[]{:S(2)}) async-start(s8[4423680]{0:T(1024)(128)(4,1)} %bitcast.196), calls=%async_computation.6 | async-start | bytes 8388608
  374.2 23.0 %slice-start.3 = ((s8[4423680]{0:T(1024)(128)(4,1)}), s8[229376]{0:T(1024)(128)(4,1)S(1)}, s32[]{:S(2)}) async-start(s8[4423680]{0:T(1024)(128)(4,1)} %bitcast.196), calls=%async_computation.7 | async-start | bytes 458752
  413.8 5.9 %copy-start.20 = (bf16[1,384,2880]{1,2,0:T(8,128)(2,1)S(1)}, bf16[1,384,2880]{1,2,0:T(8,128)(2,1)}, u32[]{:S(2)}) copy-start(bf16[1,384,2880]{1,2,0:T(8,128)(2,1)} %param.35) | copy-start | bytes 6635524
  439.7 62.9 %copy-start.4 = (f32[128,32,20]{0,1,2:T(8,128)S(1)}, f32[128,32,20]{0,1,2:T(8,128)}, u32[]{:S(2)}) copy-start(f32[128,32,20]{0,1,2:T(8,128)} %get-tuple-element.6) | copy-start | bytes 983044
  (5 other events, 4.5 us)
Sparse Core Ops, SparseCore 0:
  14.1 151.6 all-gather.6
  183.9 47.5 all-gather.4

commit v6 on v4

--- a/solution.py
+++ b/solution.py
@@ -120,14 +120,17 @@
         output_up_factors,
     )
     local_count = adapter_down_factors.shape[0]
-    joined_factors = jnp.concatenate([f.reshape(local_count, -1) for f in local_factors], axis=1)
-    all_factors = lax.all_gather(joined_factors, "dp", axis=0, tiled=True)
-    factors = []
+    rest_factors = local_factors[1:]
+    joined_factors = jnp.concatenate([f.reshape(local_count, -1) for f in rest_factors], axis=1)
+    all_down = lax.all_gather(adapter_down_factors, "dp", axis=0, tiled=True)
+    rest_gathered = lax.all_gather(joined_factors, "dp", axis=0, tiled=False)
+    adapter_total = rest_gathered.shape[0] * local_count
+    factors = [all_down]
     offset = 0
-    for f in local_factors:
+    for f in rest_factors:
         width = f.shape[1] * f.shape[2]
         factors.append(
-            all_factors[:, offset : offset + width].reshape(all_factors.shape[0], f.shape[1], f.shape[2])
+            rest_gathered[:, :, offset : offset + width].reshape(adapter_total, f.shape[1], f.shape[2])
         )
         offset += width
     all_down, all_up_query, all_up_keyval, all_o_down, all_o_up = factors

time: 524 us -> 520 us (level)
  local copies, waits for them, and re-layouts: 66.4 us -> 48.4 us
  waiting for transfers between devices: 200 us -> 214 us
    all_gather x1 -> x2, waiting for transfers between devices: 116 us -> 131 us  [the longest x1 88.1 us: shards(): all_down = lax.all_gather(adapter_down_factors, 'dp', axis=0, tiled=True)]
    unnamed x60 -> x48, local copies, waits for them, and re-layouts: 15.9 us -> 4.41 us
  transfers between devices with their start and end apart: 11 -> 12, of which waited for: 4 -> 5; matrix products, arithmetic and copies ran while one was open for 35% -> 32% of each run, Pallas kernels for 0% -> 0%
where the time goes in v6:
time: 520 us; the launch traced here: 516 us
  waiting for transfers between devices  214 us (41%)
  matrix products  115 us (22%)
  blocking collectives  88.2 us (17%)
  local copies, waits for them, and re-layouts  48.4 us (9%)
  other arithmetic  21.4 us (4%)
  starting transfers between devices  15.4 us (3%)
  between operations  14.2 us (3%)
    all_gather x1, waiting for transfers between devices, shards(): all_down = lax.all_gather(adapter_down_factors, 'dp', axis=0, tiled=True)  88.1 us
    all_to_all x1, blocking collectives, shards(): lax.all_to_all(expert_rows, 'expert', split_axis=0, concat_axis=0, tiled=...  62.9 us
    all_gather x1, waiting for transfers between devices, shards(): rest_gathered = lax.all_gather(joined_factors, 'dp', axis=0, tiled=False)  43 us
    all_to_all x1, waiting for transfers between devices, shards(): lax.all_to_all(dispatch, 'expert', split_axis=0, concat_axis=0, tiled=True)  37.5 us
    all_gather x1, waiting for transfers between devices, shards(): lax.all_gather(jnp.concatenate([key_rows, value_rows], axis=1), 'expert',...  31.9 us
    all_gather x1, blocking collectives, shards(): row_ids = lax.all_gather(prompt_number, 'expert', axis=1, tiled=True)[0]  25.3 us
    dot_general x4, matrix products, shards(): jnp.einsum('esd,fd->esf', arrived, up_w, preferred_element_type=jnp.float32)  22.5 us
    dot_general x4, matrix products, shards(): jnp.einsum('esd,fd->esf', arrived, gate_w, preferred_element_type=jnp.flo...  21 us
  transfers between devices with their start and end apart: 12, of which 5 were waited for; matrix products, arithmetic and copies ran while one was open for 32% of the time, Pallas kernels for 0%

profile of v6, /device:TPU:1, one launch (start us, length us, event | category | flops | bytes accessed | tf_op | source)
XLA Modules:
  0.0 516.1 jit_solution(888440101672268908)
XLA Ops:
  18.7 25.3 %all_gather.15 = s32[1,4096]{1,0:T(1,128)S(1)} all-gather(s32[1,128]{1,0:T(1,128)S(1)} %copy-done.14), channel_id=1, replica_groups=mesh['dp'=4,'expert'=32] {'expert'}, dimensions={1}, use_global_device_ids=true | all-gather | bytes 16896 | tf_op jit(solution)/shard_map/all_gather | solution.py:106
  49.1 43.0 %all-gather.10.cloned.1.call-done = bf16[4,4,119808]{2,1,0:T(4,128)(2,1)} async-done(((bf16[1,4,119808]{2,1,0:T(4,128)(2,1)}), bf16[4,4,119808]{2,1,0:T(4,128)(2,1)}) %all-gather.10.cloned.1.call-update) | async-done | bytes 3833872 | tf_op jit(solution)/shard_map/all_gather | solution.py:126
  93.4 88.1 %all-gather.6.cloned.1.call-done = bf16[16,48,2880]{2,1,0:T(8,128)(2,1)} async-done(((bf16[4,48,2880]{2,1,0:T(8,128)(2,1)}), bf16[16,48,2880]{2,1,0:T(8,128)(2,1)}) %all-gather.6.cloned.1.call-update) | async-done | bytes 4423696 | tf_op jit(solution)/shard_map/all_gather | solution.py:125
  181.4 3.7 fusion.54
  187.6 3.3 fusion.99
  201.8 31.9 %all-gather.8.cloned.1.call-done = bf16[4096,512]{1,0:T(8,128)(2,1)} async-done(((bf16[128,512]{1,0:T(8,128)(2,1)}), bf16[4096,512]{1,0:T(8,128)(2,1)}) %all-gather.8.cloned.1.call-update) | async-done | bytes 4194320 | tf_op jit(solution)/shard_map/all_gather | solution.py:180
  233.7 3.8 fusion.98
  237.5 4.1 copy.71
  241.6 18.1 %fusion.101 = (f32[4,8,128]{2,1,0:T(8,128)S(1)}, f32[4,8,128,2176]{2,3,1,0:T(8,128)}) fusion(bf16[128,4,8,32]{0,3,2,1:T(8,128)(2,1)} %bitcast.175, bf16[128,4,8,32]{0,3,2,1:T(8,128)(2,1)S(1)} %bitcast.174, bf16[4096,4,64]{0,2,1:T(8,128)(2,1)} %bitcast.171, s32[]{:T(128)S(6)} %min.4, pred[128,2176]{0,1:T(8,128)(4,1)S(1)} %compare_and_fusion), kind=kOutput, calls=%fused_computation.156 | convolution fusion | flops 1168633856 | bytes 37584900 | tf_op jit(solution)/shard_map/tkgd,nkd->kgtn/dot_general | solution.py:196
  259.8 13.6 %fusion = f32[4,8,128]{2,1,0:T(8,128)S(1)} fusion(f32[4,8,128,2176]{2,3,1,0:T(8,128)} %get-tuple-element.27, f32[4,8,128]{2,1,0:T(8,128)S(1)} %broadcast_maximum_fusion), kind=kLoop, calls=%fused_computation.2 | loop fusion | flops 17821696 | bytes 35684352 | tf_op jit(solution)/shard_map/reduce_sum | solution.py:206
  273.5 2.9 copy.73
  276.4 14.4 %fusion.51 = bf16[128,4,8,64]{0,3,2,1:T(8,128)(2,1)S(1)} fusion(f32[4,8,128,2176]{2,3,1,0:T(8,128)} %get-tuple-element.27, f32[4,8,128]{2,1,0:T(8,128)S(1)} %broadcast_maximum_fusion, bf16[4096,4,64]{0,2,1:T(8,128)(2,1)} %bitcast.172, s32[]{:T(128)S(6)} %min.4, f32[128,4,8]{0,2,1:T(8,128)S(1)} %get-tuple-element.20, f32[128,4,8]{0,2,1:T(8,128)S(1)} %get-tuple-element.19), kind=kOutput, calls=%fused_computation.60 | convolution fusion | flops 1159462912 | bytes 37339140 | tf_op jit(solution)/shard_map/kgtn,nkd->kgtd/dot_general | solution.py:207
  290.8 6.2 %fusion.102 = f32[128,2880]{0,1:T(8,128)S(1)} fusion(bf16[2048,2880]{0,1:T(8,128)(2,1)} %param.32, bf16[128,2048]{0,1:T(8,128)(2,1)S(1)} %bitcast.178), kind=kOutput, calls=%fused_computation.157 | convolution fusion | flops 1509949440 | bytes 13795328 | tf_op jit(solution)/shard_map/dot_general | solution.py:224
  300.6 3.3 copy.80
  303.8 5.3 %all-to-all-start = ((bf16[32,20,2880]{2,1,0:T(8,128)(2,1)}), bf16[32,20,2880]{2,1,0:T(8,128)(2,1)}, u32[]{:S(2)}, u32[]{:S(2)}) async-start(bf16[32,20,2880]{2,1,0:T(8,128)(2,1)} %copy.80), calls=%async_computation | async-start | bytes 9043968 | tf_op jit(solution)/shard_map/all_to_all | solution.py:253
  318.6 3.2 slice_bitcast_fusion.9
  322.0 3.3 slice_bitcast_fusion.8
  327.7 37.5 %all-to-all-done = bf16[32,20,2880]{2,1,0:T(8,128)(2,1)} async-done(((bf16[32,20,2880]{2,1,0:T(8,128)(2,1)}), bf16[32,20,2880]{2,1,0:T(8,128)(2,1)}, u32[]{:S(2)}, u32[]{:S(2)}) %all-to-all-start) | async-done | bytes 3686432 | tf_op jit(solution)/shard_map/all_to_all | solution.py:253
  365.2 5.2 fusion.22
  370.4 5.3 %fusion.31 = f32[32,20,384]{2,1,0:T(8,128)S(1)} fusion(bf16[32,20,2880]{2,1,0:T(8,128)(2,1)} %all-to-all-done, bf16[2,384,2880]{1,2,0:T(8,128)(2,1)} %collective-permute-done), kind=kOutput, calls=%fused_computation.38 | convolution fusion | flops 1415577600 | bytes 7716864 | tf_op jit(solution)/shard_map/esd,fd->esf/dot_general | solution.py:256
  375.7 5.2 %fusion.19 = f32[32,20,384]{2,1,0:T(8,128)S(1)} fusion(bf16[32,20,2880]{2,1,0:T(8,128)(2,1)} %all-to-all-done, bf16[2,384,2880]{1,2,0:T(8,128)(2,1)} %collective-permute-done.2), kind=kOutput, calls=%fused_computation.23 | convolution fusion | flops 1415577600 | bytes 7716864 | tf_op jit(solution)/shard_map/esd,fd->esf/dot_general | solution.py:256
  380.9 12.5 %collective-permute-done.4 = bf16[384,2880]{0,1:T(8,128)(2,1)} collective-permute-done((bf16[384,2880]{0,1:T(8,128)(2,1)}, bf16[384,2880]{0,1:T(8,128)(2,1)}, u32[]{:S(2)}, u32[]{:S(2)}) %collective-permute-start.4) | collective-permute-done | bytes 2211872 | tf_op jit(solution)/shard_map/ppermute | solution.py:68
  393.4 5.4 %fusion.25 = f32[32,20,384]{2,1,0:T(8,128)S(1)} fusion(bf16[32,20,2880]{2,1,0:T(8,128)(2,1)} %all-to-all-done, bf16[384,2880]{0,1:T(8,128)(2,1)} %collective-permute-done.4), kind=kOutput, calls=%fused_computation.32 | convolution fusion | flops 1415577600 | bytes 6881280 | tf_op jit(solution)/shard_map/esd,fd->esf/dot_general | solution.py:256
  398.8 5.1 fusion.46
  403.9 5.8 %multiply_convert_fusion.3 = bf16[32,20,384]{2,1,0:T(8,128)(2,1)S(1)} fusion(f32[32,20,384]{2,1,0:T(8,128)S(1)} %fusion.31, bf16[32,20,2880]{2,1,0:T(8,128)(2,1)} %all-to-all-done, bf16[2,384,2880]{1,2,0:T(8,128)(2,1)} %collective-permute-done), kind=kOutput, calls=%fused_computation.64 | convolution fusion | flops 1417052160 | bytes 8208384 | tf_op jit(solution)/shard_map/esd,fd->esf/dot_general | solution.py:257
  409.7 5.8 %multiply_convert_fusion.2 = bf16[32,20,384]{2,1,0:T(8,128)(2,1)S(1)} fusion(f32[32,20,384]{2,1,0:T(8,128)S(1)} %fusion.19, bf16[32,20,2880]{2,1,0:T(8,128)(2,1)} %all-to-all-done, bf16[2,384,2880]{1,2,0:T(8,128)(2,1)} %collective-permute-done.2), kind=kOutput, calls=%fused_computation.63 | convolution fusion | flops 1417052160 | bytes 8208384 | tf_op jit(solution)/shard_map/esd,fd->esf/dot_general | solution.py:257
  415.5 5.9 %multiply_convert_fusion.1 = bf16[32,20,384]{2,1,0:T(8,128)(2,1)S(1)} fusion(f32[32,20,384]{2,1,0:T(8,128)S(1)} %fusion.25, bf16[32,20,2880]{2,1,0:T(8,128)(2,1)} %all-to-all-done, bf16[384,2880]{0,1:T(8,128)(2,1)} %collective-permute-done.5), kind=kOutput, calls=%fused_computation.62 | convolution fusion | flops 1417052160 | bytes 7372800 | tf_op jit(solution)/shard_map/esd,fd->esf/dot_general | solution.py:257
  423.6 3.8 convolution_convert_fusion.1
  427.6 5.9 %convolution_convert_fusion = bf16[32,20,2880]{2,0,1:T(8,128)(2,1)} fusion(bf16[384,2880]{0,1:T(8,128)(2,1)} %collective-permute-done.3, bf16[32,20,384]{2,1,0:T(8,128)(2,1)S(1)} %multiply_convert_fusion.2), kind=kOutput, calls=%fused_computation.8 | convolution fusion | flops 1417420800 | bytes 6389760 | tf_op jit(solution)/shard_map/esf,fd->esd/dot_general | solution.py:262
  436.0 4.2 add_convert_fusion
  441.3 62.9 %all_to_all.10 = bf16[32,20,2880]{2,1,0:T(8,128)(2,1)S(1)} all-to-all(bf16[32,20,2880]{2,1,0:T(8,128)(2,1)S(1)} %copy.88), channel_id=1, replica_groups=mesh['dp'=4,'expert'=32] {'expert'}, dimensions={0} | all-to-all | bytes 7372800 | tf_op jit(solution)/shard_map/all_to_all | solution.py:271
  504.2 4.9 fusion.16
  (137 shorter events, 53.2 us)
Async XLA Ops:
  6.5 85.6 %all-gather.10.cloned.1.call-start = ((), (), s32[]{:S(2)}) async-start(), calls=%async_computation.4 | async-start | bytes 4792320 | tf_op jit(solution)/shard_map/all_gather | solution.py:126
  9.1 9.3 %copy-start.13 = (s32[128,4]{0,1:T(4,128)S(1)}, s32[128,4]{0,1:T(4,128)}, u32[]{:S(2)}) copy-start(s32[128,4]{0,1:T(4,128)} %param.36) | copy-start | bytes 6148
  10.2 8.5 %copy-start.14 = (s32[1,128]{1,0:T(1,128)S(1)}, s32[1,128]{1,0:T(1,128)}, u32[]{:S(2)}) copy-start(s32[1,128]{1,0:T(1,128)} %param.23) | copy-start | bytes 1540
  10.3 34.2 %copy-start.16 = (f32[32]{0:T(128)S(1)}, f32[32]{0:T(128)}, u32[]{:S(2)}) copy-start(f32[32]{0:T(128)} %param.25) | copy-start | bytes 388
  11.2 35.8 %copy-start.17 = (s32[1,16]{1,0:T(1,128)S(1)}, s32[1,16]{1,0:T(1,128)}, u32[]{:S(2)}) copy-start(s32[1,16]{1,0:T(1,128)} %param.24) | copy-start | bytes 196
  11.2 35.9 %copy-start.1 = (bf16[128,2880]{0,1:T(8,128)(2,1)S(1)}, bf16[128,2880]{0,1:T(8,128)(2,1)}, u32[]{:S(2)}) copy-start(bf16[128,2880]{0,1:T(8,128)(2,1)} %param.19) | copy-start | bytes 2211844
  12.7 168.8 %copy-start.19 = (f32[2880]{0:T(1024)S(1)}, f32[2880]{0:T(1024)}, u32[]{:S(2)}) copy-start(f32[2880]{0:T(1024)} %param.26) | copy-start | bytes 34564
  12.7 168.8 %all-gather.6.cloned.1.call-start = ((), (), s32[]{:S(2)}) async-start(), calls=%async_computation.2 | async-start | bytes 5652480 | tf_op jit(solution)/shard_map/all_gather | solution.py:125
  13.4 220.3 %all-gather.8.cloned.1.call-start = ((), (), s32[]{:S(2)}) async-start(), calls=%async_computation.3 | async-start | bytes 4325376 | tf_op jit(solution)/shard_map/all_gather | solution.py:180
  13.5 305.1 %collective-permute-start = (bf16[2,384,2880]{1,2,0:T(8,128)(2,1)}, bf16[2,384,2880]{1,2,0:T(8,128)(2,1)}, u32[]{:S(2)}, u32[]{:S(2)}) collective-permute-start(bf16[2,384,2880]{1,2,0:T(8,128)(2,1)} %bitcast.193), channel_id=1, source_target_pairs={{0,32},{32,64},{64,96},{96,0},{1,33},{33,65},{65,97},{97,1},{2,34}... | collective-permute-start | bytes 13271048 | tf_op jit(solution)/shard_map/ppermute | solution.py:61
  15.6 306.4 %collective-permute-start.2 = (bf16[2,384,2880]{1,2,0:T(8,128)(2,1)}, bf16[2,384,2880]{1,2,0:T(8,128)(2,1)}, u32[]{:S(2)}, u32[]{:S(2)}) collective-permute-start(bf16[2,384,2880]{1,2,0:T(8,128)(2,1)} %bitcast.194), channel_id=1, source_target_pairs={{0,96},{32,0},{64,32},{96,64},{1,97},{33,1},{65,33},{97,65},{2,98}... | collective-permute-start | bytes 13271048 | tf_op jit(solution)/shard_map/ppermute | solution.py:62
  16.9 292.3 %collective-permute-start.3 = (bf16[384,2880]{0,1:T(8,128)(2,1)}, bf16[384,2880]{0,1:T(8,128)(2,1)}, u32[]{:S(2)}, u32[]{:S(2)}) collective-permute-start(bf16[384,2880]{0,1:T(8,128)(2,1)} %bitcast.199), channel_id=1, source_target_pairs={{0,96},{32,0},{64,32},{96,64},{1,97},{33,1},{65,33},{97,65},{2,98}... | collective-permute-start | bytes 6635528 | tf_op jit(solution)/shard_map/ppermute | solution.py:62
  18.3 297.1 %collective-permute-start.1 = (bf16[384,2880]{0,1:T(8,128)(2,1)}, bf16[384,2880]{0,1:T(8,128)(2,1)}, u32[]{:S(2)}, u32[]{:S(2)}) collective-permute-start(bf16[384,2880]{0,1:T(8,128)(2,1)} %bitcast.200), channel_id=1, source_target_pairs={{0,32},{32,64},{64,96},{96,0},{1,33},{33,65},{65,97},{97,1},{2,34}... | collective-permute-start | bytes 6635528 | tf_op jit(solution)/shard_map/ppermute | solution.py:61
  47.7 137.8 %copy-start.5 = (f32[128,32]{0,1:T(8,128)}, f32[128,32]{0,1:T(8,128)S(1)}, u32[]{:S(2)}) copy-start(f32[128,32]{0,1:T(8,128)S(1)} %get-tuple-element.24) | copy-start | bytes 49156
  47.7 137.8 %copy-start.7 = (f32[128,32]{0,1:T(8,128)}, f32[128,32]{0,1:T(8,128)S(1)}, u32[]{:S(2)}) copy-start(f32[128,32]{0,1:T(8,128)S(1)} %get-tuple-element.25) | copy-start | bytes 49156
  93.3 91.8 %copy-start.10 = (bf16[128,256]{1,0:T(8,128)(2,1)S(1)}, bf16[128,256]{1,0:T(8,128)(2,1)}, u32[]{:S(2)}) copy-start(bf16[128,256]{1,0:T(8,128)(2,1)} %param.21) | copy-start | bytes 196612
  93.4 92.3 %copy-start.9 = (bf16[128,256]{1,0:T(8,128)(2,1)S(1)}, bf16[128,256]{1,0:T(8,128)(2,1)}, u32[]{:S(2)}) copy-start(bf16[128,256]{1,0:T(8,128)(2,1)} %param.22) | copy-start | bytes 196612
  93.4 93.2 %copy-start.15 = (f32[128,4]{0,1:T(4,128)S(1)}, f32[128,4]{0,1:T(4,128)}, u32[]{:S(2)}) copy-start(f32[128,4]{0,1:T(4,128)} %param.37) | copy-start | bytes 6148
  191.6 2.7 slice-start
  196.9 4.0 copy-start.6
  196.9 4.0 copy-start.8
  241.6 18.1 %copy-start.11 = (f32[4,8]{1,0:T(4,128)S(1)}, f32[4,8]{1,0:T(4,128)}, u32[]{:S(2)}) copy-start(f32[4,8]{1,0:T(4,128)} %broadcast_in_dim.14) | copy-start | bytes 388
  290.8 6.2 %copy-start.3 = (bf16[16,16,2048]{2,1,0:T(8,128)(2,1)S(1)}, bf16[16,16,2048]{2,1,0:T(8,128)(2,1)}, u32[]{:S(2)}) copy-start(bf16[16,16,2048]{2,1,0:T(8,128)(2,1)} %dot_general.84) | copy-start | bytes 3145732
  303.8 61.4 %all-to-all-start = ((bf16[32,20,2880]{2,1,0:T(8,128)(2,1)}), bf16[32,20,2880]{2,1,0:T(8,128)(2,1)}, u32[]{:S(2)}, u32[]{:S(2)}) async-start(bf16[32,20,2880]{2,1,0:T(8,128)(2,1)} %copy.80), calls=%async_computation | async-start | bytes 9043968 | tf_op jit(solution)/shard_map/all_to_all | solution.py:253
  313.0 120.6 %collective-permute-start.7 = (bf16[192,2880]{1,0:T(8,128)(2,1)}, bf16[192,2880]{1,0:T(8,128)(2,1)}, u32[]{:S(2)}, u32[]{:S(2)}) collective-permute-start(bf16[192,2880]{1,0:T(8,128)(2,1)} %copy.86), channel_id=1, source_target_pairs={{0,96},{32,0},{64,32},{96,64},{1,97},{33,1},{65,33},{97,65},{2,98}... | collective-permute-start | bytes 3317768 | tf_op jit(solution)/shard_map/ppermute | solution.py:69
  318.6 117.4 %collective-permute-start.6 = (bf16[192,2880]{1,0:T(8,128)(2,1)}, bf16[192,2880]{1,0:T(8,128)(2,1)S(1)}, u32[]{:S(2)}, u32[]{:S(2)}) collective-permute-start(bf16[192,2880]{1,0:T(8,128)(2,1)} %copy.84), channel_id=1, source_target_pairs={{0,32},{32,64},{64,96},{96,0},{1,33},{33,65},{65,97},{97,1},{2,34}... | collective-permute-start | bytes 3317768 | tf_op jit(solution)/shard_map/ppermute | solution.py:68
  321.8 71.6 %collective-permute-start.4 = (bf16[384,2880]{0,1:T(8,128)(2,1)}, bf16[384,2880]{0,1:T(8,128)(2,1)}, u32[]{:S(2)}, u32[]{:S(2)}) collective-permute-start(bf16[384,2880]{0,1:T(8,128)(2,1)} %slice_bitcast_fusion.9), channel_id=1, source_target_pairs={{0,32},{32,64},{64,96},{96,0},{1,33},{33,65},{65,97},{97,1},{2,34}... | collective-permute-start | bytes 6635528 | tf_op jit(solution)/shard_map/ppermute | solution.py:68
  325.3 90.2 %collective-permute-start.5 = (bf16[384,2880]{0,1:T(8,128)(2,1)}, bf16[384,2880]{0,1:T(8,128)(2,1)}, u32[]{:S(2)}, u32[]{:S(2)}) collective-permute-start(bf16[384,2880]{0,1:T(8,128)(2,1)} %slice_bitcast_fusion.8), channel_id=1, source_target_pairs={{0,96},{32,0},{64,32},{96,64},{1,97},{33,1},{65,33},{97,65},{2,98}... | collective-permute-start | bytes 6635528 | tf_op jit(solution)/shard_map/ppermute | solution.py:69
  370.4 28.4 %slice-start.1 = ((s8[4423680]{0:T(1024)(128)(4,1)}), s8[4194304]{0:T(1024)(128)(4,1)S(1)}, s32[]{:S(2)}) async-start(s8[4423680]{0:T(1024)(128)(4,1)} %bitcast.196), calls=%async_computation.6 | async-start | bytes 8388608
  375.7 23.1 %slice-start.2 = ((s8[4423680]{0:T(1024)(128)(4,1)}), s8[229376]{0:T(1024)(128)(4,1)S(1)}, s32[]{:S(2)}) async-start(s8[4423680]{0:T(1024)(128)(4,1)} %bitcast.196), calls=%async_computation.7 | async-start | bytes 458752
  415.4 5.9 %copy-start.18 = (bf16[1,384,2880]{1,2,0:T(8,128)(2,1)S(1)}, bf16[1,384,2880]{1,2,0:T(8,128)(2,1)}, u32[]{:S(2)}) copy-start(bf16[1,384,2880]{1,2,0:T(8,128)(2,1)} %param.35) | copy-start | bytes 6635524
  441.3 62.9 %copy-start.2 = (f32[128,32,20]{0,1,2:T(8,128)S(1)}, f32[128,32,20]{0,1,2:T(8,128)}, u32[]{:S(2)}) copy-start(f32[128,32,20]{0,1,2:T(8,128)} %get-tuple-element.6) | copy-start | bytes 983044
  (3 other events, 3.2 us)
Sparse Core Ops, SparseCore 0:
  12.8 79.2 all-gather.9
  93.8 87.6 all-gather.5
  186.7 46.9 all-gather.7
